TPU v7x, 512 devices: a whole 4x4x16 slice. The times are simulated.
512 devices in a mesh: ctx: 8 (over x, z_hi), ch: 64 (over z_lo, y, core).
Axes of the slice: x: 4, y: 4, z: 16 (z_hi: 2, z_lo: 8; z = z_hi * 8 + z_lo), core: 2. Of those that a mesh axis runs over, the one named last changes fastest.
Arguments:
- first_in: bfloat16 [2048, 65536], P('ch', 'ctx'), may hold values from -6 to 6
- second_in: bfloat16 [2048, 65536], P('ch', 'ctx'), may hold values from -6 to 6
- third_in: bfloat16 [2048, 65536], P('ch', 'ctx'), may hold values from -6 to 6
- grad_heads: bfloat16 [2048, 65536], P(None, ('ctx', 'ch')), may hold values from -6 to 6
- residue: float32 [128, 16], P('ch'), may hold values from -1.5 to 1.5
- decay_rate: float32 [128, 16], P('ch'), may hold values from 3.0517578e-06 to 0.1, as said below
- skip_gain: float32 [2048], P('ch'), may hold values from -3 to 3
Outputs:
- grad_first: bfloat16 [2048, 65536], P('ch', 'ctx')
- grad_second: bfloat16 [2048, 65536], P('ch', 'ctx')
- grad_third: bfloat16 [2048, 65536], P('ch', 'ctx')
- grad_residue: float32 [128, 16], P('ch')
- grad_skip: float32 [2048], P('ch')
Inputs may be any that keep to these rules, and one draw needn't show every extreme that they name: `decay_rate`: positive decay rate of each mode.
All inputs are finite; a program needn't handle non-finite values.
Results may differ from a plain program's by a relative error of at most 0.006.
Values may be sent and summed in bfloat16 or wider, within the bound.
No kernel may reach another device: no remote copies, remote signals or barrier semaphores. Data moves between devices by JAX's collectives and lax.ppermute only.
A program may use at most 64 MiB of HBM per device.

v0:
```python
import jax
import jax.numpy as jnp
from jax import lax
from jax.sharding import PartitionSpec as P

PRECISE = lax.Precision.HIGHEST


def carried_in(array, axis, combine, identity, reverse):
    devices, place = (lax.axis_size(axis), lax.axis_index(axis))
    everything = jax.tree.map(lambda part: lax.all_gather(part, axis), array)
    start = jax.tree.map(
        lambda part, zero: jnp.broadcast_to(jnp.asarray(zero, part.dtype), part.shape),
        array,
        identity,
    )

    def step(k, before):
        at = devices - 1 - k if reverse else k
        reached = at > place if reverse else at < place
        new = combine(before, jax.tree.map(lambda part: part[at], everything))
        return jax.tree.map(lambda a, b: jnp.where(reached, a, b), new, before)

    return lax.fori_loop(0, devices, step, start)


def link_states(earlier, later):
    return (later[0] + later[1][:, None, :] * earlier[0], earlier[1] * later[1])


def on_device(first_in, second_in, third_in, grad_heads, residue, decay_rate, skip_gain):
    channels, length = first_in.shape
    groups, mode_count = residue.shape
    group_width = channels // groups
    block_len = min(512, length)
    span_count = length // block_len
    ctx_count = lax.axis_size("ctx")
    seq_total = length * ctx_count
    split_shape = (groups, group_width, span_count, block_len)
    mode_weight = residue * jnp.sqrt(2.0 * decay_rate)
    rate_col = decay_rate[:, :, None]
    rate_box = decay_rate[:, :, None, None] * block_len
    offsets = jnp.arange(block_len, dtype=jnp.float32)
    middle = offsets - float(block_len // 2)
    falling = jnp.exp(-rate_col * middle)
    rising = jnp.exp(rate_col * middle)
    lower_mask = offsets[:, None] >= offsets[None, :]
    toeplitz = jnp.einsum(
        "gri,grj->gij", mode_weight[:, :, None] * falling, rising, precision=PRECISE
    )
    toeplitz = jnp.where(lower_mask[None], toeplitz, 0.0)
    decay_in = jnp.exp(-rate_col * offsets)
    tail_decay = jnp.exp(-rate_col * (block_len - offsets))
    head_decay = jnp.exp(-rate_col * (offsets + 1.0))
    rise_modes = mode_weight[:, :, None] * decay_in
    fall_modes = mode_weight[:, :, None] * jnp.exp(-rate_col * (block_len - 1.0 - offsets))
    span_pos = jnp.arange(span_count, dtype=jnp.float32)
    later_decay = jnp.exp(-rate_col * block_len * (span_count - 1.0 - span_pos))
    start_decay = jnp.exp(-rate_col * block_len * span_pos)
    span_gap = span_pos[:, None] - 1.0 - span_pos[None, :]
    between = jnp.where(span_gap >= 0.0, jnp.exp(-rate_box * jnp.maximum(span_gap, 0.0)), 0.0)
    block_decay = jnp.exp(-decay_rate * length)
    skip_split = skip_gain.reshape(groups, group_width, 1, 1)
    gated = first_in.astype(jnp.float32) * second_in.astype(jnp.float32)
    gated_split = gated.reshape(split_shape)
    within = jnp.einsum("gcnj,gij->gcni", gated_split, toeplitz, precision=PRECISE)
    span_state = jnp.einsum("gcnj,grj->gcnr", gated_split, tail_decay, precision=PRECISE)
    fwd_local = jnp.einsum("gcnr,grn->gcr", span_state, later_decay, precision=PRECISE)
    grad_out = lax.all_to_all(grad_heads, "ch", split_axis=0, concat_axis=1, tiled=True)
    grad_conv = grad_out.astype(jnp.float32) * third_in.astype(jnp.float32)
    grad_split = grad_conv.reshape(split_shape)
    back_within = jnp.einsum("gcni,gij->gcnj", grad_split, toeplitz, precision=PRECISE)
    back_state = jnp.einsum("gcni,gri->gcnr", grad_split, head_decay, precision=PRECISE)
    bwd_local = jnp.einsum("gcnr,grn->gcr", back_state, start_decay, precision=PRECISE)
    identity = (jnp.zeros_like(fwd_local), jnp.ones_like(block_decay))
    enter_fwd = carried_in((fwd_local, block_decay), "ctx", link_states, identity, False)[0]
    enter_bwd = carried_in((bwd_local, block_decay), "ctx", link_states, identity, True)[0]
    enter_spans = jnp.einsum("grnm,gcmr->gcnr", between, span_state, precision=PRECISE)
    enter_spans = enter_spans + jnp.einsum(
        "grn,gcr->gcnr", start_decay, enter_fwd, precision=PRECISE
    )
    convolved = (
        within
        + jnp.einsum("gcnr,gri->gcni", enter_spans, rise_modes, precision=PRECISE)
        + skip_split * gated_split
    )
    grad_third = (grad_out.astype(jnp.float32) * convolved.reshape(channels, length)).astype(
        jnp.bfloat16
    )
    leave_spans = jnp.einsum("grmn,gcmr->gcnr", between, back_state, precision=PRECISE)
    leave_spans = leave_spans + jnp.einsum(
        "grn,gcr->gcnr", later_decay, enter_bwd, precision=PRECISE
    )
    grad_mixed = (
        back_within
        + jnp.einsum("gcnr,gri->gcni", leave_spans, fall_modes, precision=PRECISE)
        + skip_split * grad_split
    )
    grad_mixed = grad_mixed.reshape(channels, length)
    grad_first = (grad_mixed * second_in.astype(jnp.float32)).astype(jnp.bfloat16)
    grad_second = (grad_mixed * first_in.astype(jnp.float32)).astype(jnp.bfloat16)
    cross_sums = jnp.einsum("gcni,gcnj->gij", grad_split, gated_split, precision=PRECISE)
    cross_sums = jnp.where(lower_mask[None], cross_sums, 0.0)
    folded = jnp.einsum("gij,grj->gri", cross_sums, rising, precision=PRECISE)
    near_part = jnp.sum(folded * falling, axis=2)
    weighted = jnp.einsum("gcni,gri->gcnr", grad_split, decay_in, precision=PRECISE)
    far_part = jnp.sum(weighted * enter_spans, axis=(1, 2))
    filter_part = jnp.sqrt(2.0 * decay_rate) * (near_part + far_part)
    skip_part = jnp.sum(grad_conv * gated, axis=1)
    filter_sum, skip_sum = lax.psum((filter_part, skip_part), "ctx")
    grad_residue = filter_sum / jnp.sqrt(float(group_width * seq_total))
    grad_skip = skip_sum / jnp.sqrt(float(seq_total))
    return (grad_first, grad_second, grad_third, grad_residue, grad_skip)


def solution(mesh):
    return jax.shard_map(
        on_device,
        mesh=mesh,
        in_specs=(
            P("ch", "ctx"),
            P("ch", "ctx"),
            P("ch", "ctx"),
            P(None, ("ctx", "ch")),
            P("ch", None),
            P("ch", None),
            P("ch"),
        ),
        out_specs=(P("ch", "ctx"), P("ch", "ctx"), P("ch", "ctx"), P("ch", None), P("ch")),
        check_vma=False,
    )
```

profile of v0, /device:TPU:64, one launch (start us, length us, event | category | flops | bytes accessed | tf_op | source)
XLA Modules:
  0.0 286.1 jit_solution(615111637534072269)
XLA Ops:
  0.6 15.6 %all-to-all-start = ((bf16[64,32,128]{2,1,0:T(8,128)(2,1)}), bf16[64,32,128]{2,1,0:T(8,128)(2,1)}, u32[]{:S(2)}, u32[]{:S(2)}) async-start(bf16[64,32,128]{2,1,0:T(8,128)(2,1)} %bitcast.170), calls=%async_computation | async-start | bytes 1048576 | tf_op jit(solution)/shard_map/all_to_all | solution.py:69
  16.3 0.7 fusion.90
  17.0 0.1 multiply_exponential_fusion.9
  17.1 0.1 copy.50
  17.2 0.5 copy-done.8
  17.7 0.1 copy.51
  17.8 1.3 convert_multiply_fusion
  19.1 0.6 copy.57
  19.7 1.0 multiply_reduce_fusion.1
  20.8 0.2 copy.27
  21.0 75.4 %all-gather.2 = f32[16,16,16]{2,1,0:T(8,128)S(1)} all-gather(f32[2,16,16]{2,1,0:T(8,128)S(1)} %bitcast.173), channel_id=4, replica_groups=mesh['ctx'=8,'ch'=64] {'ctx'}, dimensions={0}, use_global_device_ids=true | all-gather | bytes 18432 | tf_op jit(solution)/shard_map/all_gather | solution.py:11
  96.3 36.9 %all-gather.3 = f32[8,2,16]{2,1,0:T(2,128)S(1)} all-gather(f32[1,2,16]{2,1,0:T(2,128)S(1)} %get-tuple-element.298), channel_id=3, replica_groups=mesh['ctx'=8,'ch'=64] {'ctx'}, dimensions={0}, use_global_device_ids=true | all-gather | bytes 1152 | tf_op jit(solution)/shard_map/all_gather | solution.py:11
  133.3 0.4 while.37
  133.7 0.1 copy.28
  133.8 0.1 mul.280
  133.9 0.4 copy-done.12
  134.3 0.2 iota_compare_fusion
  134.5 0.1 fusion.89
  134.6 0.1 fusion.88
  134.7 0.6 fusion.21
  135.3 0.7 copy-done.6
  136.0 1.0 fusion.45
  137.1 2.0 fusion.70
  139.1 2.2 fusion.18
  141.3 1.6 copy.58
  142.9 0.6 iota_subtract_fusion.2
  143.5 3.3 %multiply_reduce_fusion = (f32[32]{0:T(128)}, f32[32,8192]{1,0:T(8,128)S(1)}, bf16[32,8192]{1,0:T(8,128)(2,1)}) fusion(bf16[32,8192]{1,0:T(8,128)(2,1)S(1)} %copy-done.2, bf16[32,8192]{1,0:T(8,128)(2,1)S(1)} %copy-done.4, bf16[32,8192]{1,0:T(8,128)(2,1)} %param.13, f32[32,8192]{1,0:T(8,128)} %bitcast.162, bf16[64,32,128]{2,1,0:T(8,128)(2,1)} %all-to-all-done), kind=kLoop, calls=%fused_computation.46 | loop fusion | flops 2621408 | bytes 4718720 | tf_op jit(solution)/shard_map/reduce_sum | solution.py:109
  146.8 0.6 copy.55
  147.4 2.3 multiply_reduce_fusion.2
  149.7 1.8 copy.24
  151.5 63.5 %all-gather = f32[16,16,16]{2,1,0:T(8,128)S(1)} all-gather(f32[2,16,16]{2,1,0:T(8,128)} %bitcast.174), channel_id=2, replica_groups=mesh['ctx'=8,'ch'=64] {'ctx'}, dimensions={0}, use_global_device_ids=true | all-gather | bytes 18432 | tf_op jit(solution)/shard_map/all_gather | solution.py:11
  215.1 15.2 %while.36 = (s32[]{:T(128)}, f32[2,16,16]{2,1,0:T(8,128)S(1)}, s32[]{:T(128)}, f32[8,2,16,16]{3,2,1,0:T(8,128)S(1)}, f32[8,2,16]{2,1,0:T(2,128)}, /*index=5*/s32[]{:T(128)}, s32[]{:T(128)}, s32[]{:T(128)}, s32[]{:T(128)}) while((s32[]{:T(128)}, f32[2,16,16]{2,1,0:T(8,128)S(1)}, s32[]{:T(128)}, f32[8,2,16,16]{3,2,1,0:T(8,128)S(1)}, ...), condition=%wide.region_1.2_spmd.clone, body=%wide.region_0.1_spmd.clone.sunk | while | flops 2056 | bytes 6703 | solution.py:24
  215.1 1.2 dynamic-slice_bitcast_fusion.4
  216.3 0.7 fusion.100
  217.0 1.2 dynamic-slice_bitcast_fusion.4
  218.2 0.7 fusion.100
  218.9 1.2 dynamic-slice_bitcast_fusion.4
  220.1 0.7 fusion.100
  220.8 1.2 dynamic-slice_bitcast_fusion.4
  222.0 0.7 fusion.100
  222.7 1.2 dynamic-slice_bitcast_fusion.4
  223.9 0.7 fusion.100
  224.6 1.2 dynamic-slice_bitcast_fusion.4
  225.8 0.7 fusion.100
  226.5 1.2 dynamic-slice_bitcast_fusion.4
  227.8 0.7 fusion.100
  228.4 1.2 dynamic-slice_bitcast_fusion.4
  229.6 0.7 fusion.100
  230.3 0.1 copy.25
  230.4 1.4 fusion.22
  231.8 1.7 fusion.47
  233.5 2.8 fusion.12
  236.3 0.6 copy.56
  237.0 0.4 copy-done.3
  237.4 0.2 copy-done.5
  237.5 1.2 fusion.26
  238.7 1.8 fusion.27
  240.6 2.0 fusion.24
  242.6 1.0 fusion.32
  243.7 0.2 copy.30
  243.9 0.2 multiply_reduce_fusion.3
  244.1 40.9 %all-reduce = (f32[2,16]{1,0:T(2,128)S(1)}, f32[32]{0:T(128)S(1)}) all-reduce(f32[2,16]{1,0:T(2,128)S(1)} %add_multiply_fusion, f32[32]{0:T(128)S(1)} %copy-done.21), channel_id=1, replica_groups=mesh['ctx'=8,'ch'=64] {'ctx'}, use_global_device_ids=true, to_apply=%region_6.7 | all-reduce | flops 64 | bytes 512 | tf_op jit(solution)/shard_map/psum | solution.py:110
  285.0 0.6 broadcast_multiply_fusion
  285.6 0.5 broadcast_multiply_fusion.2
  (66 shorter events, 0.3 us)
Async XLA Ops:
  0.6 142.9 %all-to-all-start = ((bf16[64,32,128]{2,1,0:T(8,128)(2,1)}), bf16[64,32,128]{2,1,0:T(8,128)(2,1)}, u32[]{:S(2)}, u32[]{:S(2)}) async-start(bf16[64,32,128]{2,1,0:T(8,128)(2,1)} %bitcast.170), calls=%async_computation | async-start | bytes 1048576 | tf_op jit(solution)/shard_map/all_to_all | solution.py:69
  16.3 120.8 %copy-start.13 = (f32[512]{0:T(512)}, f32[512]{0:T(512)S(1)}, u32[]{:S(2)}) copy-start(f32[512]{0:T(512)S(1)} %iota_add_fusion.1) | copy-start | bytes 6148
  17.0 117.7 %copy-start.19 = (f32[2,16]{1,0:T(2,128)}, f32[2,16]{1,0:T(2,128)S(1)}, u32[]{:S(2)}) copy-start(f32[2,16]{1,0:T(2,128)S(1)} %get-tuple-element.300) | copy-start | bytes 388
  17.0 120.1 %copy-start.16 = (f32[2,16]{1,0:T(2,128)}, f32[2,16]{1,0:T(2,128)S(1)}, u32[]{:S(2)}) copy-start(f32[2,16]{1,0:T(2,128)S(1)} %get-tuple-element.296) | copy-start | bytes 388
  17.0 130.4 %copy-start.10 = (f32[2,16]{1,0:T(2,128)}, f32[2,16]{1,0:T(2,128)S(1)}, u32[]{:S(2)}) copy-start(f32[2,16]{1,0:T(2,128)S(1)} %get-tuple-element.299) | copy-start | bytes 388
  17.1 0.6 copy-start.8
  19.1 114.7 %copy-start.22 = (f32[32]{0:T(128)S(1)}, f32[32]{0:T(128)}, u32[]{:S(2)}) copy-start(f32[32]{0:T(128)} %param.17) | copy-start | bytes 388
  19.7 119.4 %copy-start = (f32[4,8,16,512]{3,2,1,0:T(8,128)}, f32[4,8,16,512]{3,2,1,0:T(8,128)S(1)}, u32[]{:S(2)}) copy-start(f32[4,8,16,512]{3,2,1,0:T(8,128)S(1)} %copy.57) | copy-start | bytes 3145732
  19.7 117.4 %copy-start.17 = (f32[2,16]{1,0:T(2,128)S(1)}, f32[2,16]{1,0:T(2,128)}, u32[]{:S(2)}) copy-start(f32[2,16]{1,0:T(2,128)} %param.16) | copy-start | bytes 388
  133.7 0.6 copy-start.12
  134.3 4.8 %copy-start.20 = (f32[2,16]{1,0:T(2,128)}, f32[2,16]{1,0:T(2,128)S(1)}, u32[]{:S(2)}) copy-start(f32[2,16]{1,0:T(2,128)S(1)} %mul.280) | copy-start | bytes 388
  134.6 0.7 copy-start.15
  134.7 0.7 copy-start.9
  135.3 0.7 copy-start.6
  141.3 2.2 copy-start.2
  141.3 2.2 copy-start.4
  236.3 1.0 copy-start.3
  236.3 1.2 copy-start.5
  237.0 1.7 copy-start.1
  238.7 1.9 copy-start.11
  238.7 1.9 copy-start.14
  238.7 1.9 copy-start.18
  240.6 3.2 %copy-start.7 = (f32[2,16,16,16]{2,1,3,0:T(8,128)S(1)}, f32[2,16,16,16]{2,1,3,0:T(8,128)}, u32[]{:S(2)}) copy-start(f32[2,16,16,16]{2,1,3,0:T(8,128)} %copy-done.6) | copy-start | bytes 98308
  240.6 3.5 %copy-start.21 = (f32[32]{0:T(128)S(1)}, f32[32]{0:T(128)}, u32[]{:S(2)}) copy-start(f32[32]{0:T(128)} %get-tuple-element.291) | copy-start | bytes 388
where the time goes:
time: 287 us; the launch traced here: 286 us
  blocking collectives  217 us (76%)
  matrix products  20 us (7%)
  local copies, waits for them, and re-layouts  18 us (6%)
  starting transfers between devices  15.6 us (5%)
  other arithmetic  14.4 us (5%)
    all_gather x3, blocking collectives, carried_in(): everything = jax.tree.map(lambda part: lax.all_gather(part, axis), array)  176 us
    psum x1, blocking collectives, on_device(): filter_sum, skip_sum = lax.psum((filter_part, skip_part), 'ctx')  40.9 us
    all_to_all x1, starting transfers between devices, on_device(): lax.all_to_all(grad_heads, 'ch', split_axis=0, concat_axis=1, tiled=True)  15.6 us
    mul x16, local copies, waits for them, and re-layouts, link_states(): return (later[0] + later[1][:, None, :] * earlier[0], earlier[1] * later[1])  9.79 us
    unnamed x52, local copies, waits for them, and re-layouts  5.87 us
  transfers between devices with their start and end apart: 1, of which 0 were waited for; matrix products, arithmetic and copies ran while one was open for 4% of the time, Pallas kernels for 0%

commit v1 on v0

v1 whole, which is shorter than its diff:
```python
import jax
import jax.numpy as jnp
from jax import lax
from jax.experimental import pallas as pl
from jax.experimental.pallas import tpu as pltpu
from jax.sharding import PartitionSpec as P

F32, BF16 = jnp.float32, jnp.bfloat16
SPAN = 128
SPANS = 64
GROUPS, WIDTH, MODES = 2, 16, 16
ROWS = SPANS * WIDTH
LENGTH = SPAN * SPANS
CTX = 8
TOKENS = LENGTH * CTX


def iota(shape, dim):
    return lax.broadcasted_iota(jnp.int32, shape, dim)


def high(x):
    return x.astype(BF16)


def low(x):
    return (x - x.astype(BF16).astype(F32)).astype(BF16)


def dot(a, b):
    return jnp.dot(a, b, preferred_element_type=F32)


def halves(x):
    return x[:, :128] + x[:, 128:]


def state_matrix(a_row, age):
    decay = jnp.exp(-a_row * age)
    lane_group = (iota((128, 128), 1) % 32) // MODES
    out = []
    for g in range(GROUPS):
        mine = jnp.where(lane_group == g, decay, 0.0)
        block = jnp.concatenate([high(mine), low(mine)], axis=1)
        out += [block, block]
    return jnp.concatenate(out, axis=0)


def mode_matrix(a_col, w_col, age):
    wave = w_col * jnp.exp(-a_col * age)
    row = iota((128, 128), 0)
    part = jnp.where(row < 64, wave.astype(BF16).astype(F32), low(wave).astype(F32))
    row_group = (row % 32) // MODES
    return jnp.concatenate(
        [jnp.where(row_group == g, part, 0.0).astype(BF16) for g in range(GROUPS)], axis=1
    )


def quad_split(x, lane):
    top = x.astype(BF16).astype(F32)
    return jnp.where((lane // 32) % 2 == 0, top, x - top).astype(BF16)


def toeplitz(a_s, w_s, g, gap):
    near = jnp.maximum(gap, 0).astype(F32)
    total = jnp.zeros((SPAN, SPAN), F32)
    for r in range(MODES):
        total = total + w_s[g, r] * jnp.exp(-a_s[g, r] * near)
    total = jnp.where(gap >= 0, total, 0.0)
    block = jnp.concatenate([high(total), low(total)], axis=1)
    return jnp.concatenate([block, block], axis=0)


def forward_kernel(
    first, second, a_row, a_col, w_col, a_s, w_s, skip,
    x_cat, x_turn, conv, enter, block_state, head_mat, near_mat, rise_j, back_toep, rise_mat, fall_mat, start_decay, later_decay,
    states, toep,
):
    a = a_row[...]
    row = iota((128, 128), 0)
    col = iota((128, 128), 1)
    token = row.astype(F32)
    lane_token = col.astype(F32)
    head_mat[...] = state_matrix(a, token + 1.0)
    near_mat[...] = state_matrix(a, token - 64.0)
    rise_j[...] = jnp.exp(a * (token - 64.0))
    rise_mat[...] = mode_matrix(a_col[...], w_col[...], lane_token)
    fall_mat[...] = mode_matrix(a_col[...], w_col[...], 127.0 - lane_token)
    n_row = iota((SPANS, 128), 0).astype(F32)
    start_decay[...] = jnp.exp(-a * (128.0 * n_row))
    later_decay[...] = jnp.exp(-a * (128.0 * (SPANS - 1.0 - n_row)))
    for g in range(GROUPS):
        toep[g] = toeplitz(a_s, w_s, g, col - row)
        back_toep[g] = toeplitz(a_s, w_s, g, row - col)
    for n in range(SPANS):
        at, here = pl.ds(n * WIDTH, WIDTH), pl.ds(n * SPAN, SPAN)
        x = first[:, here].astype(F32) * second[:, here].astype(F32)
        hi, lo = high(x), low(x)
        for g in range(GROUPS):
            c = slice(g * WIDTH, (g + 1) * WIDTH)
            x_cat[at, pl.ds(256 * g, 128)] = hi[c]
            x_cat[at, pl.ds(256 * g + 128, 128)] = lo[c]
    states[...] = halves(dot(x_cat[...], state_matrix(a, 128.0 - token)))
    step = jnp.exp(-a * 128.0)
    carry = jnp.zeros((WIDTH, 128), F32)
    for n in range(SPANS):
        at = pl.ds(n * WIDTH, WIDTH)
        enter[at, :] = carry
        carry = carry * step + states[at, :]
    block_state[...] = carry
    lane = iota((ROWS, 128), 1)
    conv[...] = dot(quad_split(enter[...], lane), rise_mat[...])
    for g in range(GROUPS):
        mine = pl.ds(256 * g, 256)
        here = pl.ds(128 * g, 128)
        x = x_cat[:, mine]
        gain = jnp.concatenate([skip[g]] * SPANS, axis=0)
        gated = x[:, :128].astype(F32) + x[:, 128:].astype(F32)
        conv[:, here] = conv[:, here] + halves(dot(x, toep[g])) + gain * gated
        x_turn[g] = x.T


def middle_kernel(
    grad_out, third, x_cat, x_turn, enter, block_state, head_mat, near_mat, rise_j, a_row,
    payload, g_cat, leave,
    states,
):
    a = a_row[...]
    total = jnp.zeros((GROUPS * WIDTH, SPAN), F32)
    for n in range(SPANS):
        at, here = pl.ds(n * WIDTH, WIDTH), pl.ds(n * SPAN, SPAN)
        y = grad_out[n].astype(F32) * third[:, here].astype(F32)
        hi, lo = high(y), low(y)
        x = []
        for g in range(GROUPS):
            c = slice(g * WIDTH, (g + 1) * WIDTH)
            g_cat[at, pl.ds(256 * g, 128)] = hi[c]
            g_cat[at, pl.ds(256 * g + 128, 128)] = lo[c]
            x.append(
                x_cat[at, pl.ds(256 * g, 128)].astype(F32)
                + x_cat[at, pl.ds(256 * g + 128, 128)].astype(F32)
            )
        total = total + y * jnp.concatenate(x, axis=0)
    states[...] = halves(dot(g_cat[...], head_mat[...]))
    row = iota((128, 128), 0)
    col = iota((128, 128), 1)
    cross = []
    for g in range(GROUPS):
        four = dot(x_turn[g], g_cat[:, pl.ds(256 * g, 256)])
        four = halves(four[:128] + four[128:])
        four = jnp.where(col >= row, four, 0.0)
        cross += [high(four), low(four)]
    near = halves(dot(jnp.concatenate(cross, axis=1), near_mat[...])) * rise_j[...]
    near = jnp.sum(near.reshape(16, 8, 128), axis=0)
    step = jnp.exp(-a * 128.0)
    carry = jnp.zeros((WIDTH, 128), F32)
    far = jnp.zeros((WIDTH, 128), F32)
    for n in reversed(range(SPANS)):
        at = pl.ds(n * WIDTH, WIDTH)
        leave[at, :] = carry
        now = states[at, :]
        far = far + now * enter[at, :]
        carry = carry * step + now
    weight = near + (far[:8] + far[8:]) * jnp.exp(a)
    direct = lax.dot_general(
        jnp.ones((8, SPAN), F32),
        jnp.concatenate([total] * 4, axis=0),
        (((1,), (1,)), ((), ())),
        precision=lax.Precision.HIGHEST,
        preferred_element_type=F32,
    )
    quarter = iota((8, 128), 1) // 32
    back = jnp.where(
        quarter == 0, carry[:8], jnp.where(quarter == 1, carry[8:], jnp.where(quarter == 2, weight, direct))
    )
    ahead = jnp.where(quarter == 0, block_state[:8, :], block_state[8:, :])
    for k in range(CTX):
        payload[k, :8, :] = back
        payload[k, 8:, :] = ahead


def backward_kernel(g_cat, leave, back_toep, fall_mat, skip, a_row, place, mixed, from_later, from_earlier):
    lane = iota((ROWS, 128), 1)
    mixed[...] = dot(quad_split(leave[...], lane), fall_mat[...])
    for g in range(GROUPS):
        here = pl.ds(128 * g, 128)
        y = g_cat[:, pl.ds(256 * g, 256)]
        gain = jnp.concatenate([skip[g]] * SPANS, axis=0)
        grad_conv = y[:, :128].astype(F32) + y[:, 128:].astype(F32)
        mixed[:, here] = mixed[:, here] + halves(dot(y, back_toep[g])) + gain * grad_conv
    a = jnp.broadcast_to(a_row[...], (8, 128)) * float(LENGTH)
    states = iota((8, 128), 1) < 64
    me = place[0]
    for k in range(CTX):
        after = jnp.maximum(k - me - 1, 0).astype(F32)
        before = jnp.maximum(me - 1 - k, 0).astype(F32)
        later = jnp.where(k > me, 1.0, 0.0)
        earlier = jnp.where(k < me, 1.0, 0.0)
        from_later[k] = jnp.where(states, jnp.exp(-a * after) * later, 1.0)
        from_earlier[k] = jnp.exp(-a * before) * earlier


def finish_kernel(
    parts, conv, mixed, grad_out, first, second, rise_mat, fall_mat, start_decay, later_decay, from_later, from_earlier, a_row,
    grad_first, grad_second, grad_third, grad_residue, grad_skip,
    left, result,
):
    a = a_row[...]
    quarter = iota((8, 128), 1) // 32
    back = jnp.zeros((8, 128), F32)
    ahead = jnp.zeros((8, 128), F32)
    running = jnp.zeros((8, 128), F32)
    far = jnp.zeros((8, 128), F32)
    block_step = jnp.exp(-a * float(LENGTH))
    for k in range(CTX):
        later, earlier = parts[k, :8, :], parts[k, 8:, :]
        back = back + later * from_later[k]
        ahead = ahead + earlier * from_earlier[k]
        far = far + later * running
        running = running * block_step + earlier

    def spread(x, q):
        x = jnp.where(quarter == q, x, 0.0)
        x = x + pltpu.roll(x, 32, 1)
        return x + pltpu.roll(x, 64, 1)

    def rows(x):
        return jnp.concatenate([spread(x, 0), spread(x, 1)], axis=0)

    lane = iota((ROWS, 128), 1)

    def fix(x, decay, matrix):
        whole = decay[...].reshape(SPANS, 1, 128) * x.reshape(1, WIDTH, 128)
        left[...] = quad_split(whole.reshape(ROWS, 128), lane)
        return dot(left[...], matrix[...])

    result[...] = conv[...] + fix(rows(ahead), start_decay, rise_mat)
    for n in range(SPANS):
        at, here = pl.ds(n * WIDTH, WIDTH), pl.ds(n * SPAN, SPAN)
        full = jnp.concatenate([result[at, pl.ds(0, 128)], result[at, pl.ds(128, 128)]], axis=0)
        grad_third[:, here] = (grad_out[n].astype(F32) * full).astype(BF16)
    result[...] = mixed[...] + fix(rows(back), later_decay, fall_mat)
    for n in range(SPANS):
        at, here = pl.ds(n * WIDTH, WIDTH), pl.ds(n * SPAN, SPAN)
        full = jnp.concatenate([result[at, pl.ds(0, 128)], result[at, pl.ds(128, 128)]], axis=0)
        grad_first[:, here] = (full * second[:, here].astype(F32)).astype(BF16)
        grad_second[:, here] = (full * first[:, here].astype(F32)).astype(BF16)
    near = spread(back, 2)
    crossed = (spread(far, 0) + spread(far, 1)) * jnp.exp(a)
    weight = jnp.sum(near + crossed, axis=0, keepdims=True)
    weight = weight * jnp.sqrt(2.0 * a) * (1.0 / (float(WIDTH * TOKENS) ** 0.5))
    grad_residue[0:1, :] = weight[:, :MODES]
    grad_residue[1:2, :] = pltpu.roll(weight, 128 - MODES, 1)[:, :MODES]
    direct = pltpu.roll(back, 32, 1)[0:1] * (1.0 / (float(TOKENS) ** 0.5))
    grad_skip[...] = direct[:, : GROUPS * WIDTH]


def call(kernel, outs, scratch, args, scalars=()):
    specs = [
        pl.BlockSpec(memory_space=pltpu.SMEM if i in scalars else pltpu.VMEM) for i in range(len(args))
    ]
    return pl.pallas_call(
        kernel,
        out_shape=tuple(jax.ShapeDtypeStruct(s, d) for s, d in outs),
        in_specs=specs,
        out_specs=tuple(pl.BlockSpec(memory_space=pltpu.VMEM) for _ in outs),
        scratch_shapes=[pltpu.VMEM(s, d) for s, d in scratch],
        compiler_params=pltpu.CompilerParams(vmem_limit_bytes=40 << 20),
    )(*args)


def prepare(residue, decay_rate, skip_gain):
    weight = residue * jnp.sqrt(2.0 * decay_rate)
    a_row = jnp.tile(decay_rate.reshape(1, 32), (1, 4))
    a_col = jnp.tile(decay_rate.reshape(32, 1), (4, 1))
    w_col = jnp.tile(weight.reshape(32, 1), (4, 1))
    return a_row, a_col, w_col, weight, skip_gain.reshape(GROUPS, WIDTH, 1)


def run_forward(first, second, a_row, a_col, w_col, a_s, w_s, skip):
    return call(
        forward_kernel,
        [
            ((ROWS, 512), BF16), ((GROUPS, 256, ROWS), BF16), ((ROWS, 256), F32), ((ROWS, 128), F32), ((WIDTH, 128), F32),
            ((512, 256), BF16), ((512, 256), BF16), ((128, 128), F32), ((GROUPS, 256, 256), BF16),
            ((128, 256), BF16), ((128, 256), BF16), ((SPANS, 128), F32), ((SPANS, 128), F32),
        ],
        [((ROWS, 128), F32), ((GROUPS, 256, 256), BF16)],
        (first, second, a_row, a_col, w_col, a_s, w_s, skip),
        scalars=(5, 6),
    )


def local(first, second, third, grad_out, exchange, residue, decay_rate, skip_gain, place):
    a_row, a_col, w_col, weight, skip = prepare(residue, decay_rate, skip_gain)
    (
        x_cat, x_turn, conv, enter, block_state, head_mat, near_mat, rise_j, back_toep,
        rise_mat, fall_mat, start_decay, later_decay,
    ) = run_forward(first, second, a_row, a_col, w_col, decay_rate, weight, skip)
    payload, g_cat, leave = call(
        middle_kernel,
        [((CTX, 16, 128), F32), ((ROWS, 512), BF16), ((ROWS, 128), F32)],
        [((ROWS, 128), F32)],
        (grad_out, third, x_cat, x_turn, enter, block_state, head_mat, near_mat, rise_j, a_row),
    )
    parts = exchange(payload)
    mixed, from_later, from_earlier = call(
        backward_kernel,
        [((ROWS, 256), F32), ((CTX, 8, 128), F32), ((CTX, 8, 128), F32)],
        [],
        (g_cat, leave, back_toep, fall_mat, skip, a_row, place),
        scalars=(6,),
    )
    shape = ((GROUPS * WIDTH, LENGTH), BF16)
    grad_first, grad_second, grad_third, grad_residue, grad_skip = call(
        finish_kernel,
        [shape, shape, shape, ((GROUPS, MODES), F32), ((1, GROUPS * WIDTH), F32)],
        [((ROWS, 128), BF16), ((ROWS, 256), F32)],
        (
            parts, conv, mixed, grad_out, first, second, rise_mat, fall_mat, start_decay, later_decay,
            from_later, from_earlier, a_row,
        ),
    )
    return grad_first, grad_second, grad_third, grad_residue, grad_skip.reshape(GROUPS * WIDTH)


def on_device(first, second, third, grad_heads, residue, decay_rate, skip_gain):
    grad_out = lax.all_to_all(
        grad_heads.reshape(SPANS, GROUPS * WIDTH, SPAN), "ch", split_axis=0, concat_axis=0, tiled=True
    )
    place = lax.axis_index("ctx").astype(jnp.int32).reshape(1)

    def exchange(payload):
        return lax.all_to_all(payload, "ctx", split_axis=0, concat_axis=0, tiled=True)

    return local(first, second, third, grad_out, exchange, residue, decay_rate, skip_gain, place)


def solution(mesh):
    return jax.shard_map(
        on_device,
        mesh=mesh,
        in_specs=(
            P("ch", "ctx"),
            P("ch", "ctx"),
            P("ch", "ctx"),
            P(None, ("ctx", "ch")),
            P("ch", None),
            P("ch", None),
            P("ch"),
        ),
        out_specs=(P("ch", "ctx"), P("ch", "ctx"), P("ch", "ctx"), P("ch", None), P("ch")),
        check_vma=False,
    )
```

time: 287 us -> 85.1 us (0.30)
  the two profiles are of different devices: /device:TPU:64 before, /device:TPU:1 now
where the time goes in v1:
time: 85.1 us; the launch traced here: 84.3 us
  starting transfers between devices  27.1 us (32%)
  local copies, waits for them, and re-layouts  25.1 us (29%)
  waiting for transfers between devices  24.4 us (29%)
  Pallas kernels  6.91 us (8%)
    unnamed x74, local copies, waits for them, and re-layouts  22.7 us
    all_to_all x1, starting transfers between devices, on_device(): lax.all_to_all(grad_heads.reshape(SPANS, GROUPS * WIDTH, SPAN), 'ch', spl...  17.4 us
    all_to_all x1, waiting for transfers between devices, on_device(): lax.all_to_all(grad_heads.reshape(SPANS, GROUPS * WIDTH, SPAN), 'ch', spl...  14 us
    all_to_all x1, waiting for transfers between devices, exchange(): lax.all_to_all(payload, 'ctx', split_axis=0, concat_axis=0, tiled=True)  10.4 us
    all_to_all x1, starting transfers between devices, exchange(): lax.all_to_all(payload, 'ctx', split_axis=0, concat_axis=0, tiled=True)  9.77 us
    pallas_call x4, Pallas kernels, call(): pl.pallas_call(kernel, out_shape=tuple((jax.ShapeDtypeStruct(s, d) for s,...  6.91 us
  transfers between devices with their start and end apart: 2, of which 2 were waited for; matrix products, arithmetic and copies ran while one was open for 3% of the time, Pallas kernels for 4%

profile of v1, /device:TPU:1, one launch (start us, length us, event | category | flops | bytes accessed | tf_op | source)
XLA Modules:
  0.0 84.3 jit_solution(17698060552571959903)
XLA Ops:
  0.6 0.0 copy-start
  0.6 0.0 copy-start.1
  0.7 17.4 %all-to-all-start = ((bf16[64,32,128]{2,1,0:T(8,128)(2,1)}), bf16[64,32,128]{2,1,0:T(8,128)(2,1)S(1)}, u32[]{:S(2)}, u32[]{:S(2)}) async-start(bf16[64,32,128]{2,1,0:T(8,128)(2,1)} %bitcast.3), calls=%async_computation | async-start | bytes 1048576 | tf_op jit(solution)/shard_map/all_to_all | solution.py:328
  18.0 0.8 tile.26
  18.8 0.6 tile.28.a_row
  19.4 0.0 copy-start.31
  19.4 0.0 copy-start.35
  19.4 0.1 tile.33.a_col
  19.5 0.6 copy-done.31
  20.1 0.0 copy-done.35
  20.1 0.0 copy-start.33
  20.1 0.1 tile.30
  20.2 0.5 copy-done.33
  20.7 0.0 copy-start.36
  20.7 0.7 tile.34.w_col
  21.4 0.0 copy-done.36
  21.4 0.1 reshape.44.skip
  21.5 0.0 copy-done
  21.5 0.0 copy-done.1
  21.5 0.0 copy-start.17
  21.5 0.8 copy-done.17
  22.4 0.0 copy-start.26
  22.4 0.7 copy-done.26
  23.0 0.0 copy-start.32
  23.0 0.7 copy-done.32
  23.7 0.0 copy-start.34
  23.7 0.7 copy-done.34
  24.4 0.0 copy-start.8
  24.4 2.6 %shard_map.110 = (bf16[1024,512]{1,0:T(8,128)(2,1)S(1)}, bf16[2,256,1024]{2,1,0:T(8,128)(2,1)S(1)}, f32[1024,256]{1,0:T(8,128)S(1)}, f32[1024,128]{1,0:T(8,128)S...) custom-call(bf16[32,8192]{1,0:T(8,128)(2,1)S(1)} %copy-done, ...), custom_call_target="tpu_custom_call" | custom-call | tf_op jit(solution)/shard_map/pallas_call | solution.py:262
  27.0 0.0 copy-start.2
  27.0 1.0 %copy-done.2 = bf16[2,256,1024]{2,1,0:T(8,128)(2,1)} copy-done((bf16[2,256,1024]{2,1,0:T(8,128)(2,1)}, bf16[2,256,1024]{2,1,0:T(8,128)(2,1)S(1)}, u32[]{:S(2)}) %copy-start.2) | copy-done | bytes 1048600
  28.0 1.0 %copy-done.6 = f32[1024,256]{1,0:T(8,128)} copy-done((f32[1024,256]{1,0:T(8,128)}, f32[1024,256]{1,0:T(8,128)S(1)}, u32[]{:S(2)}) %copy-start.6) | copy-done | bytes 1048600
  29.0 0.8 copy-done.11
  29.8 0.7 copy-done.13
  30.5 0.7 copy-done.15
  31.2 0.6 copy-done.18
  31.8 0.6 copy-done.20
  32.4 0.6 copy-done.22
  33.0 0.6 copy-done.24
  33.6 0.6 copy-done.29
  34.2 14.0 %all-to-all-done.grad_out = bf16[64,32,128]{2,1,0:T(8,128)(2,1)S(1)} async-done(((bf16[64,32,128]{2,1,0:T(8,128)(2,1)}), bf16[64,32,128]{2,1,0:T(8,128)(2,1)S(1)}, u32[]{:S(2)}, u32[]{:S(2)}) %all-to-all-start) | async-done | bytes 524320 | tf_op jit(solution)/shard_map/all_to_all | solution.py:328
  48.2 0.0 copy-done.8
  48.2 0.7 copy-done.30
  48.9 0.0 copy-done.27
  48.9 1.2 %copy-done.3 = bf16[2,256,1024]{2,1,0:T(8,128)(2,1)S(1)} copy-done((bf16[2,256,1024]{2,1,0:T(8,128)(2,1)S(1)}, bf16[2,256,1024]{2,1,0:T(8,128)(2,1)}, u32[]{:S(2)}) %copy-start.3) | copy-done | bytes 1048600
  50.1 1.0 %copy-done.12 = f32[1024,128]{1,0:T(8,128)S(1)} copy-done((f32[1024,128]{1,0:T(8,128)S(1)}, f32[1024,128]{1,0:T(8,128)}, u32[]{:S(2)}) %copy-start.12) | copy-done | bytes 524312
  51.2 0.9 %copy-done.14 = bf16[512,256]{1,0:T(8,128)(2,1)S(1)} copy-done((bf16[512,256]{1,0:T(8,128)(2,1)S(1)}, bf16[512,256]{1,0:T(8,128)(2,1)}, u32[]{:S(2)}) %copy-start.14) | copy-done | bytes 262168
  52.1 0.9 %copy-done.16 = bf16[512,256]{1,0:T(8,128)(2,1)S(1)} copy-done((bf16[512,256]{1,0:T(8,128)(2,1)S(1)}, bf16[512,256]{1,0:T(8,128)(2,1)}, u32[]{:S(2)}) %copy-start.16) | copy-done | bytes 262168
  53.1 0.8 copy-done.21
  53.9 1.6 %shard_map.111 = (f32[8,16,128]{2,1,0:T(8,128)}, bf16[1024,512]{1,0:T(8,128)(2,1)S(1)}, f32[1024,128]{1,0:T(8,128)S(1)}) custom-call(bf16[64,32,128]{2,1,0:T(8,128)(2,1)S(1)} %all-to-all-done.grad_out, bf16[32,8192]{1,0:T(8,128)(2,1)S(1)} %copy-done.8, bf16[1024,512]{1,0:T(8,128)(2,1)S(1)} %get-tuple-element.29.x_cat, bf16[2,256,1024]{2,1,0:T(8,128)(2,1)S(1)} %copy-done.3, ...), custom_call_target="tpu_custom_call" | custom-call | tf_op jit(solution)/shard_map/pallas_call | solution.py:262
  55.6 1.0 %copy-done.4 = bf16[1024,512]{1,0:T(8,128)(2,1)} copy-done((bf16[1024,512]{1,0:T(8,128)(2,1)}, bf16[1024,512]{1,0:T(8,128)(2,1)S(1)}, u32[]{:S(2)}) %copy-start.4) | copy-done | bytes 1048600
  56.5 0.8 copy-done.9
  57.3 9.8 %all-to-all-start.1 = ((f32[8,16,128]{2,1,0:T(8,128)}), f32[8,16,128]{2,1,0:T(8,128)S(1)}, u32[]{:S(2)}, u32[]{:S(2)}) async-start(f32[8,16,128]{2,1,0:T(8,128)} %get-tuple-element.36), calls=%async_computation.1 | async-start | bytes 131072 | tf_op jit(solution)/shard_map/all_to_all | solution.py:334
  67.1 0.7 copy-done.28
  67.8 1.2 %copy-done.5 = bf16[1024,512]{1,0:T(8,128)(2,1)S(1)} copy-done((bf16[1024,512]{1,0:T(8,128)(2,1)S(1)}, bf16[1024,512]{1,0:T(8,128)(2,1)}, u32[]{:S(2)}) %copy-start.5) | copy-done | bytes 1048600
  69.0 1.0 %copy-done.10 = f32[1024,128]{1,0:T(8,128)S(1)} copy-done((f32[1024,128]{1,0:T(8,128)S(1)}, f32[1024,128]{1,0:T(8,128)}, u32[]{:S(2)}) %copy-start.10) | copy-done | bytes 524312
  70.0 0.6 shard_map.112
  70.6 10.4 %all-to-all-done.1.parts = f32[8,16,128]{2,1,0:T(8,128)S(1)} async-done(((f32[8,16,128]{2,1,0:T(8,128)}), f32[8,16,128]{2,1,0:T(8,128)S(1)}, u32[]{:S(2)}, u32[]{:S(2)}) %all-to-all-start.1) | async-done | bytes 65568 | tf_op jit(solution)/shard_map/all_to_all | solution.py:334
  81.0 0.0 copy-done.19
  81.0 0.0 copy-done.23
  81.0 0.0 copy-done.25
  81.0 0.0 copy-start.7
  81.0 1.2 %copy-done.7 = f32[1024,256]{1,0:T(8,128)S(1)} copy-done((f32[1024,256]{1,0:T(8,128)S(1)}, f32[1024,256]{1,0:T(8,128)}, u32[]{:S(2)}) %copy-start.7) | copy-done | bytes 1048600
  82.3 2.1 %shard_map.113 = (bf16[32,8192]{1,0:T(8,128)(2,1)}, bf16[32,8192]{1,0:T(8,128)(2,1)}, bf16[32,8192]{1,0:T(8,128)(2,1)}, f32[2,16]{1,0:T(2,128)}, f32[1,32]{1,0:T(1,128)}) custom-call(f32[8,16,128]{2,1,0:T(8,128)S(1)} %all-to-all-done.1.parts, f32[1024,256]{1,0:T(8,128)S(1)} %copy-done.7, f32[1024,256]{1,0:T(8,128)S(1)} %get-tuple-element.42.mixed, ...), custom_call_target="tpu_custom_call" | custom-call | tf_op jit(solution)/shard_map/pallas_call | solution.py:262
  (27 shorter events, 0.1 us)
Async XLA Ops:
  0.6 20.9 %copy-start = (bf16[32,8192]{1,0:T(8,128)(2,1)S(1)}, bf16[32,8192]{1,0:T(8,128)(2,1)}, u32[]{:S(2)}) copy-start(bf16[32,8192]{1,0:T(8,128)(2,1)} %first.3) | copy-start | bytes 1572868
  0.6 20.9 %copy-start.1 = (bf16[32,8192]{1,0:T(8,128)(2,1)S(1)}, bf16[32,8192]{1,0:T(8,128)(2,1)}, u32[]{:S(2)}) copy-start(bf16[32,8192]{1,0:T(8,128)(2,1)} %second.3) | copy-start | bytes 1572868
  0.7 47.5 %all-to-all-start = ((bf16[64,32,128]{2,1,0:T(8,128)(2,1)}), bf16[64,32,128]{2,1,0:T(8,128)(2,1)S(1)}, u32[]{:S(2)}, u32[]{:S(2)}) async-start(bf16[64,32,128]{2,1,0:T(8,128)(2,1)} %bitcast.3), calls=%async_computation | async-start | bytes 1048576 | tf_op jit(solution)/shard_map/all_to_all | solution.py:328
  19.4 0.7 copy-start.31
  19.4 0.7 copy-start.35
  20.1 0.6 copy-start.33
  20.7 0.7 copy-start.36
  21.5 0.8 copy-start.17
  22.4 0.7 copy-start.26
  23.0 0.7 copy-start.32
  23.7 0.7 copy-start.34
  24.4 23.8 %copy-start.8 = (bf16[32,8192]{1,0:T(8,128)(2,1)S(1)}, bf16[32,8192]{1,0:T(8,128)(2,1)}, u32[]{:S(2)}) copy-start(bf16[32,8192]{1,0:T(8,128)(2,1)} %third.1) | copy-start | bytes 1572868
  27.0 1.0 %copy-start.2 = (bf16[2,256,1024]{2,1,0:T(8,128)(2,1)}, bf16[2,256,1024]{2,1,0:T(8,128)(2,1)S(1)}, u32[]{:S(2)}) copy-start(bf16[2,256,1024]{2,1,0:T(8,128)(2,1)S(1)} %get-tuple-element.30.x_turn) | copy-start | bytes 3145732
  28.0 1.0 %copy-start.6 = (f32[1024,256]{1,0:T(8,128)}, f32[1024,256]{1,0:T(8,128)S(1)}, u32[]{:S(2)}) copy-start(f32[1024,256]{1,0:T(8,128)S(1)} %get-tuple-element.37.conv) | copy-start | bytes 3145732
  29.0 0.8 copy-start.11
  29.8 0.7 copy-start.13
  30.5 0.7 copy-start.15
  31.2 0.6 copy-start.18
  31.8 0.6 copy-start.20
  32.4 0.6 copy-start.22
  33.0 0.6 copy-start.24
  33.6 0.6 copy-start.29
  48.2 0.7 copy-start.30
  48.2 0.7 copy-start.27
  48.9 1.2 %copy-start.3 = (bf16[2,256,1024]{2,1,0:T(8,128)(2,1)S(1)}, bf16[2,256,1024]{2,1,0:T(8,128)(2,1)}, u32[]{:S(2)}) copy-start(bf16[2,256,1024]{2,1,0:T(8,128)(2,1)} %copy-done.2) | copy-start | bytes 3145732
  50.1 1.0 %copy-start.12 = (f32[1024,128]{1,0:T(8,128)S(1)}, f32[1024,128]{1,0:T(8,128)}, u32[]{:S(2)}) copy-start(f32[1024,128]{1,0:T(8,128)} %copy-done.11) | copy-start | bytes 1572868
  51.2 0.9 %copy-start.14 = (bf16[512,256]{1,0:T(8,128)(2,1)S(1)}, bf16[512,256]{1,0:T(8,128)(2,1)}, u32[]{:S(2)}) copy-start(bf16[512,256]{1,0:T(8,128)(2,1)} %copy-done.13) | copy-start | bytes 786436
  52.1 0.9 %copy-start.16 = (bf16[512,256]{1,0:T(8,128)(2,1)S(1)}, bf16[512,256]{1,0:T(8,128)(2,1)}, u32[]{:S(2)}) copy-start(bf16[512,256]{1,0:T(8,128)(2,1)} %copy-done.15) | copy-start | bytes 786436
  53.1 0.8 copy-start.21
  55.6 1.0 %copy-start.4 = (bf16[1024,512]{1,0:T(8,128)(2,1)}, bf16[1024,512]{1,0:T(8,128)(2,1)S(1)}, u32[]{:S(2)}) copy-start(bf16[1024,512]{1,0:T(8,128)(2,1)S(1)} %get-tuple-element.38.g_cat) | copy-start | bytes 3145732
  56.5 0.8 copy-start.9
  57.3 23.7 %all-to-all-start.1 = ((f32[8,16,128]{2,1,0:T(8,128)}), f32[8,16,128]{2,1,0:T(8,128)S(1)}, u32[]{:S(2)}, u32[]{:S(2)}) async-start(f32[8,16,128]{2,1,0:T(8,128)} %get-tuple-element.36), calls=%async_computation.1 | async-start | bytes 131072 | tf_op jit(solution)/shard_map/all_to_all | solution.py:334
  67.1 0.7 copy-start.28
  67.8 1.2 %copy-start.5 = (bf16[1024,512]{1,0:T(8,128)(2,1)S(1)}, bf16[1024,512]{1,0:T(8,128)(2,1)}, u32[]{:S(2)}) copy-start(bf16[1024,512]{1,0:T(8,128)(2,1)} %copy-done.4) | copy-start | bytes 3145732
  69.0 1.0 %copy-start.10 = (f32[1024,128]{1,0:T(8,128)S(1)}, f32[1024,128]{1,0:T(8,128)}, u32[]{:S(2)}) copy-start(f32[1024,128]{1,0:T(8,128)} %copy-done.9) | copy-start | bytes 1572868
  70.0 11.0 %copy-start.19 = (bf16[128,256]{1,0:T(8,128)(2,1)S(1)}, bf16[128,256]{1,0:T(8,128)(2,1)}, u32[]{:S(2)}) copy-start(bf16[128,256]{1,0:T(8,128)(2,1)} %copy-done.18) | copy-start | bytes 196612
  70.0 11.0 %copy-start.23 = (f32[64,128]{1,0:T(8,128)S(1)}, f32[64,128]{1,0:T(8,128)}, u32[]{:S(2)}) copy-start(f32[64,128]{1,0:T(8,128)} %copy-done.22) | copy-start | bytes 98308
  70.0 11.0 %copy-start.25 = (f32[64,128]{1,0:T(8,128)S(1)}, f32[64,128]{1,0:T(8,128)}, u32[]{:S(2)}) copy-start(f32[64,128]{1,0:T(8,128)} %copy-done.24) | copy-start | bytes 98308
  81.0 1.2 %copy-start.7 = (f32[1024,256]{1,0:T(8,128)S(1)}, f32[1024,256]{1,0:T(8,128)}, u32[]{:S(2)}) copy-start(f32[1024,256]{1,0:T(8,128)} %copy-done.6) | copy-start | bytes 3145732

commit v2 on v1

v2 whole, which is shorter than its diff:
```python
import jax
import jax.numpy as jnp
from jax import lax
from jax.experimental import pallas as pl
from jax.experimental.pallas import tpu as pltpu
from jax.sharding import PartitionSpec as P

F32, BF16 = jnp.float32, jnp.bfloat16
SPAN = 128
SPANS = 64
GROUPS, WIDTH, MODES = 2, 16, 16
ROWS = SPANS * WIDTH
LENGTH = SPAN * SPANS
CTX = 8
TOKENS = LENGTH * CTX


def iota(shape, dim):
    return lax.broadcasted_iota(jnp.int32, shape, dim)


def high(x):
    return x.astype(BF16)


def low(x):
    return (x - x.astype(BF16).astype(F32)).astype(BF16)


def dot(a, b):
    return jnp.dot(a, b, preferred_element_type=F32)


def halves(x):
    return x[:, :128] + x[:, 128:]


def state_matrix(a_row, age):
    decay = jnp.exp(-a_row * age)
    lane_group = (iota((128, 128), 1) % 32) // MODES
    out = []
    for g in range(GROUPS):
        mine = jnp.where(lane_group == g, decay, 0.0)
        block = jnp.concatenate([high(mine), low(mine)], axis=1)
        out += [block, block]
    return jnp.concatenate(out, axis=0)


def mode_matrix(a_col, w_col, age):
    wave = w_col * jnp.exp(-a_col * age)
    row = iota((128, 128), 0)
    part = jnp.where(row < 64, wave.astype(BF16).astype(F32), low(wave).astype(F32))
    row_group = (row % 32) // MODES
    return jnp.concatenate(
        [jnp.where(row_group == g, part, 0.0).astype(BF16) for g in range(GROUPS)], axis=1
    )


def quad_split(x, lane):
    top = x.astype(BF16).astype(F32)
    return jnp.where((lane // 32) % 2 == 0, top, x - top).astype(BF16)


def toeplitz(a_s, w_s, g, gap):
    near = jnp.maximum(gap, 0).astype(F32)
    total = jnp.zeros((SPAN, SPAN), F32)
    for r in range(MODES):
        total = total + w_s[g, r] * jnp.exp(-a_s[g, r] * near)
    total = jnp.where(gap >= 0, total, 0.0)
    block = jnp.concatenate([high(total), low(total)], axis=1)
    return jnp.concatenate([block, block], axis=0)


def begin(pairs, sems, first=0):
    copies = [
        pltpu.make_async_copy(source, target, sems.at[first + i]) for i, (source, target) in enumerate(pairs)
    ]
    for copy in copies:
        copy.start()
    return copies


def finish(copies):
    for copy in copies:
        copy.wait()


def forward_kernel(
    first_hbm, second_hbm, a_row, a_col, w_col, a_s, w_s, skip,
    x_cat_hbm, x_turn_hbm, conv_hbm, enter_hbm, back_toep_hbm, mats_hbm,
    first, second, x_cat, x_turn, conv, enter, back_toep, mats, states, toep, sems,
):
    inputs = begin([(first_hbm, first), (second_hbm, second)], sems)
    a = a_row[...]
    row = iota((128, 128), 0)
    col = iota((128, 128), 1)
    token = row.astype(F32)
    lane_token = col.astype(F32)
    mats[0] = mode_matrix(a_col[...], w_col[...], lane_token)
    mats[1] = mode_matrix(a_col[...], w_col[...], 127.0 - lane_token)
    for g in range(GROUPS):
        toep[g] = toeplitz(a_s, w_s, g, col - row)
        back_toep[g] = toeplitz(a_s, w_s, g, row - col)
    outputs = begin([(back_toep, back_toep_hbm), (mats, mats_hbm)], sems, 2)
    finish(inputs)
    for n in range(SPANS):
        at, here = pl.ds(n * WIDTH, WIDTH), pl.ds(n * SPAN, SPAN)
        x = first[:, here].astype(F32) * second[:, here].astype(F32)
        hi, lo = high(x), low(x)
        for g in range(GROUPS):
            c = slice(g * WIDTH, (g + 1) * WIDTH)
            x_cat[at, pl.ds(256 * g, 128)] = hi[c]
            x_cat[at, pl.ds(256 * g + 128, 128)] = lo[c]
    outputs += begin([(x_cat, x_cat_hbm)], sems, 4)
    states[...] = halves(dot(x_cat[...], state_matrix(a, 128.0 - token)))
    step = jnp.exp(-a * 128.0)
    carry = jnp.zeros((WIDTH, 128), F32)
    for n in range(SPANS):
        at = pl.ds(n * WIDTH, WIDTH)
        enter[at, :] = carry
        carry = carry * step + states[at, :]
    enter[pl.ds(ROWS, WIDTH), :] = carry
    enter[pl.ds(ROWS + WIDTH, 8), :] = jnp.broadcast_to(a, (8, 128))
    outputs += begin([(enter, enter_hbm)], sems, 5)
    lane = iota((ROWS, 128), 1)
    conv[...] = dot(quad_split(enter[pl.ds(0, ROWS), :], lane), mats[0])
    for g in range(GROUPS):
        mine = pl.ds(256 * g, 256)
        here = pl.ds(128 * g, 128)
        x = x_cat[:, mine]
        gain = jnp.concatenate([skip[g]] * SPANS, axis=0)
        gated = x[:, :128].astype(F32) + x[:, 128:].astype(F32)
        conv[:, here] = conv[:, here] + halves(dot(x, toep[g])) + gain * gated
        x_turn[g] = x.T
    outputs += begin([(x_turn, x_turn_hbm), (conv, conv_hbm)], sems, 6)
    finish(outputs)


def middle_kernel(
    grad_out, third_hbm, x_cat_hbm, x_turn_hbm, enter_hbm,
    payload_hbm, grad_out_hbm,
    third, x_cat, x_turn, enter, g_cat, states, payload, sems,
):
    early = begin([(third_hbm, third)], sems)
    enter_in, turn_in, cat_in = begin(
        [(enter_hbm, enter), (x_turn_hbm, x_turn), (x_cat_hbm, x_cat)], sems, 1
    )
    outputs = begin([(grad_out, grad_out_hbm)], sems, 4)
    row = iota((128, 128), 0)
    col = iota((128, 128), 1)
    token = row.astype(F32)
    finish(early)
    for n in range(SPANS):
        at, here = pl.ds(n * WIDTH, WIDTH), pl.ds(n * SPAN, SPAN)
        y = grad_out[n].astype(F32) * third[:, here].astype(F32)
        hi, lo = high(y), low(y)
        for g in range(GROUPS):
            c = slice(g * WIDTH, (g + 1) * WIDTH)
            g_cat[at, pl.ds(256 * g, 128)] = hi[c]
            g_cat[at, pl.ds(256 * g + 128, 128)] = lo[c]
    finish([enter_in])
    a = enter[pl.ds(ROWS + WIDTH, 1), :]
    states[...] = halves(dot(g_cat[...], state_matrix(a, token + 1.0)))
    finish([turn_in])
    cross = []
    for g in range(GROUPS):
        four = dot(x_turn[g], g_cat[:, pl.ds(256 * g, 256)])
        four = halves(four[:128] + four[128:])
        four = jnp.where(col >= row, four, 0.0)
        cross += [high(four), low(four)]
    near = halves(dot(jnp.concatenate(cross, axis=1), state_matrix(a, token - 64.0)))
    near = near * jnp.exp(a * (token - 64.0))
    near = jnp.sum(near.reshape(16, 8, 128), axis=0)
    step = jnp.exp(-a * 128.0)
    carry = jnp.zeros((WIDTH, 128), F32)
    far = jnp.zeros((WIDTH, 128), F32)
    for n in reversed(range(SPANS)):
        at = pl.ds(n * WIDTH, WIDTH)
        now = states[at, :]
        far = far + now * enter[at, :]
        carry = carry * step + now
    weight = near + (far[:8] + far[8:]) * jnp.exp(a)
    finish([cat_in])
    total = []
    for g in range(GROUPS):
        mine = jnp.zeros((WIDTH, SPAN), F32)
        hi, lo = pl.ds(256 * g, 128), pl.ds(256 * g + 128, 128)
        for n in range(SPANS):
            at = pl.ds(n * WIDTH, WIDTH)
            x = x_cat[at, hi].astype(F32) + x_cat[at, lo].astype(F32)
            y = g_cat[at, hi].astype(F32) + g_cat[at, lo].astype(F32)
            mine = mine + x * y
        total.append(mine)
    direct = lax.dot_general(
        jnp.ones((8, SPAN), F32),
        jnp.concatenate(total * 4, axis=0),
        (((1,), (1,)), ((), ())),
        precision=lax.Precision.HIGHEST,
        preferred_element_type=F32,
    )
    quarter = iota((8, 128), 1) // 32
    back = jnp.where(
        quarter == 0, carry[:8], jnp.where(quarter == 1, carry[8:], jnp.where(quarter == 2, weight, direct))
    )
    state = enter[pl.ds(ROWS, WIDTH), :]
    ahead = jnp.where(quarter == 0, state[:8, :], state[8:, :])
    for k in range(CTX):
        payload[k, :8, :] = back
        payload[k, 8:, :] = ahead
    finish(outputs + begin([(payload, payload_hbm)], sems, 5))


def backward_kernel(
    grad_out_hbm, third_hbm, back_toep_hbm, mats_hbm, a_row, skip, place, payload_hbm,
    mixed_hbm, small_hbm,
    grad_out, third, back_toep, mats, g_cat, states, leave, mixed, small, sems,
):
    early = begin(
        [(grad_out_hbm, grad_out), (third_hbm, third), (back_toep_hbm, back_toep), (mats_hbm, mats)], sems
    )
    a = a_row[...]
    token = iota((128, 128), 0).astype(F32)
    wide = jnp.broadcast_to(a, (8, 128)) * float(LENGTH)
    is_state = iota((8, 128), 1) < 64
    me = place[0]
    for k in range(CTX):
        after = jnp.maximum(k - me - 1, 0).astype(F32)
        before = jnp.maximum(me - 1 - k, 0).astype(F32)
        later = jnp.where(k > me, 1.0, 0.0)
        earlier = jnp.where(k < me, 1.0, 0.0)
        small[k] = jnp.where(is_state, jnp.exp(-wide * after) * later, 1.0)
        small[CTX + k] = jnp.exp(-wide * before) * earlier
    small[2 * CTX] = jnp.broadcast_to(a, (8, 128))
    outputs = begin([(small, small_hbm)], sems, 4)
    finish(early)
    for n in range(SPANS):
        at, here = pl.ds(n * WIDTH, WIDTH), pl.ds(n * SPAN, SPAN)
        y = grad_out[n].astype(F32) * third[:, here].astype(F32)
        hi, lo = high(y), low(y)
        for g in range(GROUPS):
            c = slice(g * WIDTH, (g + 1) * WIDTH)
            g_cat[at, pl.ds(256 * g, 128)] = hi[c]
            g_cat[at, pl.ds(256 * g + 128, 128)] = lo[c]
    states[...] = halves(dot(g_cat[...], state_matrix(a, token + 1.0)))
    step = jnp.exp(-a * 128.0)
    carry = jnp.zeros((WIDTH, 128), F32)
    for n in reversed(range(SPANS)):
        at = pl.ds(n * WIDTH, WIDTH)
        leave[at, :] = carry
        carry = carry * step + states[at, :]
    lane = iota((ROWS, 128), 1)
    mixed[...] = dot(quad_split(leave[...], lane), mats[1])
    for g in range(GROUPS):
        here = pl.ds(128 * g, 128)
        y = g_cat[:, pl.ds(256 * g, 256)]
        gain = jnp.concatenate([skip[g]] * SPANS, axis=0)
        grad_conv = y[:, :128].astype(F32) + y[:, 128:].astype(F32)
        mixed[:, here] = mixed[:, here] + halves(dot(y, back_toep[g])) + gain * grad_conv
    outputs += begin([(mixed, mixed_hbm)], sems, 5)
    finish(outputs)


CHUNKS = 4
CHUNK_SPANS = SPANS // CHUNKS
CHUNK_ROWS = ROWS // CHUNKS
CHUNK_TOKENS = LENGTH // CHUNKS


def finish_kernel(
    parts, small_hbm, mats_hbm, conv_hbm, mixed_hbm, grad_out_hbm, first_hbm, second_hbm,
    grad_first_hbm, grad_second_hbm, grad_third_hbm, grad_residue_hbm, grad_skip_hbm,
    small, mats, conv, mixed, grad_out, first, second, grad_first, grad_second, grad_third, grad_residue, grad_skip, decays,
    sems,
):
    def rows_of(c):
        return pl.ds(c * CHUNK_ROWS, CHUNK_ROWS)

    def spans_of(c):
        return pl.ds(c * CHUNK_SPANS, CHUNK_SPANS)

    def tokens_of(c):
        return pl.ds(c * CHUNK_TOKENS, CHUNK_TOKENS)

    early = begin([(small_hbm, small), (mats_hbm, mats)], sems)
    used = 2
    third_in, gate_in = [], []
    for c in range(CHUNKS):
        third_in.append(
            begin(
                [
                    (conv_hbm.at[rows_of(c), :], conv.at[rows_of(c), :]),
                    (grad_out_hbm.at[spans_of(c)], grad_out.at[spans_of(c)]),
                ],
                sems,
                used,
            )
        )
        used += 2
    for c in range(CHUNKS):
        gate_in.append(
            begin(
                [
                    (mixed_hbm.at[rows_of(c), :], mixed.at[rows_of(c), :]),
                    (first_hbm.at[:, tokens_of(c)], first.at[:, tokens_of(c)]),
                    (second_hbm.at[:, tokens_of(c)], second.at[:, tokens_of(c)]),
                ],
                sems,
                used,
            )
        )
        used += 3
    finish(early)
    a = small[2 * CTX, 0:1, :]
    quarter = iota((8, 128), 1) // 32
    back = jnp.zeros((8, 128), F32)
    ahead = jnp.zeros((8, 128), F32)
    running = jnp.zeros((8, 128), F32)
    far = jnp.zeros((8, 128), F32)
    block_step = jnp.exp(-a * float(LENGTH))
    for k in range(CTX):
        later, earlier = parts[k, :8, :], parts[k, 8:, :]
        back = back + later * small[k]
        ahead = ahead + earlier * small[CTX + k]
        far = far + later * running
        running = running * block_step + earlier

    def spread(x, q):
        x = jnp.where(quarter == q, x, 0.0)
        x = x + pltpu.roll(x, 32, 1)
        return x + pltpu.roll(x, 64, 1)

    def rows(x):
        return jnp.concatenate([spread(x, 0), spread(x, 1)], axis=0)

    span = iota((SPANS, 128), 0).astype(F32)
    decays[0] = jnp.exp(-a * (128.0 * span))
    decays[1] = jnp.exp(-a * (128.0 * (SPANS - 1.0 - span)))
    lane = iota((CHUNK_ROWS, 128), 1)

    def fix(x, side, c):
        decay = decays[side, spans_of(c), :].reshape(CHUNK_SPANS, 1, 128)
        whole = (decay * x.reshape(1, WIDTH, 128)).reshape(CHUNK_ROWS, 128)
        return dot(quad_split(whole, lane), mats[side])

    def channels(x, i):
        x = x[i * WIDTH : (i + 1) * WIDTH]
        return jnp.concatenate([x[:, :128], x[:, 128:]], axis=0)

    outputs = []
    entering, leaving = rows(ahead), rows(back)
    for c in range(CHUNKS):
        add = fix(entering, 0, c)
        finish(third_in[c])
        full = conv[rows_of(c), :] + add
        for i in range(CHUNK_SPANS):
            n = c * CHUNK_SPANS + i
            grad_third[:, pl.ds(n * SPAN, SPAN)] = (grad_out[n].astype(F32) * channels(full, i)).astype(BF16)
        outputs += begin([(grad_third.at[:, tokens_of(c)], grad_third_hbm.at[:, tokens_of(c)])], sems, used)
        used += 1
    near = spread(back, 2)
    crossed = (spread(far, 0) + spread(far, 1)) * jnp.exp(a)
    weight = jnp.sum(near + crossed, axis=0, keepdims=True)
    weight = weight * jnp.sqrt(2.0 * a) * (1.0 / (float(WIDTH * TOKENS) ** 0.5))
    grad_residue[0:1, :] = weight[:, :MODES]
    grad_residue[1:2, :] = pltpu.roll(weight, 128 - MODES, 1)[:, :MODES]
    direct = pltpu.roll(back, 32, 1)[0:1] * (1.0 / (float(TOKENS) ** 0.5))
    grad_skip[...] = direct[:, : GROUPS * WIDTH]
    outputs += begin([(grad_residue, grad_residue_hbm), (grad_skip, grad_skip_hbm)], sems, used)
    used += 2
    for c in range(CHUNKS):
        add = fix(leaving, 1, c)
        finish(gate_in[c])
        full = mixed[rows_of(c), :] + add
        for i in range(CHUNK_SPANS):
            here = pl.ds((c * CHUNK_SPANS + i) * SPAN, SPAN)
            part = channels(full, i)
            grad_first[:, here] = (part * second[:, here].astype(F32)).astype(BF16)
            grad_second[:, here] = (part * first[:, here].astype(F32)).astype(BF16)
        outputs += begin(
            [
                (grad_first.at[:, tokens_of(c)], grad_first_hbm.at[:, tokens_of(c)]),
                (grad_second.at[:, tokens_of(c)], grad_second_hbm.at[:, tokens_of(c)]),
            ],
            sems,
            used,
        )
        used += 2
    finish(outputs)


FINISH_COPIES = 2 + 5 * CHUNKS + 3 * CHUNKS + 2


def call(kernel, outs, scratch, copies, args, vmem=(), smem=()):
    def space(i):
        return pltpu.VMEM if i in vmem else pltpu.SMEM if i in smem else pltpu.HBM

    return pl.pallas_call(
        kernel,
        out_shape=tuple(pltpu.HBM(s, d) for s, d in outs),
        in_specs=[pl.BlockSpec(memory_space=space(i)) for i in range(len(args))],
        out_specs=tuple(pl.BlockSpec(memory_space=pltpu.HBM) for _ in outs),
        scratch_shapes=[pltpu.VMEM(s, d) for s, d in scratch] + [pltpu.SemaphoreType.DMA((copies,))],
        compiler_params=pltpu.CompilerParams(vmem_limit_bytes=40 << 20),
    )(
        *(
            pltpu.with_memory_space_constraint(x, pltpu.HBM) if space(i) == pltpu.HBM else x
            for i, x in enumerate(args)
        )
    )


def prepare(residue, decay_rate, skip_gain):
    weight = residue * jnp.sqrt(2.0 * decay_rate)
    a_row = jnp.tile(decay_rate.reshape(1, 32), (1, 4))
    a_col = jnp.tile(decay_rate.reshape(32, 1), (4, 1))
    w_col = jnp.tile(weight.reshape(32, 1), (4, 1))
    return a_row, a_col, w_col, weight, skip_gain.reshape(GROUPS, WIDTH, 1)


GATE = ((GROUPS * WIDTH, LENGTH), BF16)
ARRIVED = ((SPANS, GROUPS * WIDTH, SPAN), BF16)
CAT = ((ROWS, 512), BF16)
TURN = ((GROUPS, 256, ROWS), BF16)
WHOLE = ((ROWS, 256), F32)
STATES = ((ROWS, 128), F32)
ENTER = ((ROWS + WIDTH + 8, 128), F32)
TOEP = ((GROUPS, 256, 256), BF16)
MATS = ((2, 128, 256), BF16)
PARTS = ((CTX, 16, 128), F32)
SMALL = ((2 * CTX + 1, 8, 128), F32)
RESIDUE = ((GROUPS, MODES), F32)
SKIP = ((1, GROUPS * WIDTH), F32)


def local(first, second, third, grad_out, exchange, residue, decay_rate, skip_gain, place):
    a_row, a_col, w_col, weight, skip = prepare(residue, decay_rate, skip_gain)
    outs = [CAT, TURN, WHOLE, ENTER, TOEP, MATS]
    x_cat, x_turn, conv, enter, back_toep, mats = call(
        forward_kernel,
        outs,
        [GATE, GATE] + outs + [STATES, TOEP],
        8,
        (first, second, a_row, a_col, w_col, decay_rate, weight, skip),
        vmem=(2, 3, 4, 7),
        smem=(5, 6),
    )
    payload, grad_out = call(
        middle_kernel,
        [PARTS, ARRIVED],
        [GATE, CAT, TURN, ENTER, CAT, STATES, PARTS],
        6,
        (grad_out, third, x_cat, x_turn, enter),
        vmem=(0,),
    )
    parts = exchange(payload)
    mixed, small = call(
        backward_kernel,
        [WHOLE, SMALL],
        [ARRIVED, GATE, TOEP, MATS, CAT, STATES, STATES, WHOLE, SMALL],
        6,
        (grad_out, third, back_toep, mats, a_row, skip, place, payload),
        vmem=(4, 5),
        smem=(6,),
    )
    outs = [GATE, GATE, GATE, RESIDUE, SKIP]
    grad_first, grad_second, grad_third, grad_residue, grad_skip = call(
        finish_kernel,
        outs,
        [SMALL, MATS, WHOLE, WHOLE, ARRIVED, GATE, GATE] + outs + [((2, SPANS, 128), F32)],
        FINISH_COPIES,
        (parts, small, mats, conv, mixed, grad_out, first, second),
        vmem=(0,),
    )
    return grad_first, grad_second, grad_third, grad_residue, grad_skip.reshape(GROUPS * WIDTH)


def on_device(first, second, third, grad_heads, residue, decay_rate, skip_gain):
    grad_out = lax.all_to_all(
        grad_heads.reshape(SPANS, GROUPS * WIDTH, SPAN), "ch", split_axis=0, concat_axis=0, tiled=True
    )
    place = lax.axis_index("ctx").astype(jnp.int32).reshape(1)

    def exchange(payload):
        return lax.all_to_all(payload, "ctx", split_axis=0, concat_axis=0, tiled=True)

    return local(first, second, third, grad_out, exchange, residue, decay_rate, skip_gain, place)


def solution(mesh):
    return jax.shard_map(
        on_device,
        mesh=mesh,
        in_specs=(
            P("ch", "ctx"),
            P("ch", "ctx"),
            P("ch", "ctx"),
            P(None, ("ctx", "ch")),
            P("ch", None),
            P("ch", None),
            P("ch"),
        ),
        out_specs=(P("ch", "ctx"), P("ch", "ctx"), P("ch", "ctx"), P("ch", None), P("ch")),
        check_vma=False,
    )
```

time: 85.1 us -> 80.1 us (0.941)
  local copies, waits for them, and re-layouts: 25.1 us -> 1.68 us
  Pallas kernels: 6.91 us -> 16.7 us
  waiting for transfers between devices: 24.4 us -> 33.7 us
    unnamed x74 -> x6, local copies, waits for them, and re-layouts: 22.7 us -> 1.12 us
    all_to_all x1, waiting for transfers between devices: 14 us -> 23.8 us  [on_device(): lax.all_to_all(grad_heads.reshape(SPANS, GROUPS * WIDTH, SPAN), 'ch', spl...]
    pallas_call x4, Pallas kernels: 6.91 us -> 16.7 us  [call(): pl.pallas_call(kernel, out_shape=tuple((pltpu.HBM(s, d) for s, d in outs)...]
    another operation x3, local copies, waits for them, and re-layouts: 1.36 us -> 0.17 us  [prepare(): a_row = jnp.tile(decay_rate.reshape(1, 32), (1, 4))]
  transfers between devices with their start and end apart: 2 -> 2, of which waited for: 2 -> 2; matrix products, arithmetic and copies ran while one was open for 3% -> 1% of each run, Pallas kernels for 4% -> 11%
where the time goes in v2:
time: 80.1 us; the launch traced here: 79.8 us
  waiting for transfers between devices  33.7 us (42%)
  starting transfers between devices  27 us (34%)
  Pallas kernels  16.7 us (21%)
  local copies, waits for them, and re-layouts  1.68 us (2%)
    all_to_all x1, waiting for transfers between devices, on_device(): lax.all_to_all(grad_heads.reshape(SPANS, GROUPS * WIDTH, SPAN), 'ch', spl...  23.8 us
    all_to_all x1, starting transfers between devices, on_device(): lax.all_to_all(grad_heads.reshape(SPANS, GROUPS * WIDTH, SPAN), 'ch', spl...  17.2 us
    pallas_call x4, Pallas kernels, call(): pl.pallas_call(kernel, out_shape=tuple((pltpu.HBM(s, d) for s, d in outs)...  16.7 us
    all_to_all x1, waiting for transfers between devices, exchange(): lax.all_to_all(payload, 'ctx', split_axis=0, concat_axis=0, tiled=True)  9.94 us
    all_to_all x1, starting transfers between devices, exchange(): lax.all_to_all(payload, 'ctx', split_axis=0, concat_axis=0, tiled=True)  9.78 us
  transfers between devices with their start and end apart: 2, of which 2 were waited for; matrix products, arithmetic and copies ran while one was open for 1% of the time, Pallas kernels for 11%

profile of v2, /device:TPU:1, one launch (start us, length us, event | category | flops | bytes accessed | tf_op | source)
XLA Modules:
  0.0 79.8 jit_solution(2262387672653031448)
XLA Ops:
  0.6 0.0 copy-start
  0.6 17.2 %all-to-all-start = ((bf16[64,32,128]{2,1,0:T(8,128)(2,1)}), bf16[64,32,128]{2,1,0:T(8,128)(2,1)S(1)}, u32[]{:S(2)}, u32[]{:S(2)}) async-start(bf16[64,32,128]{2,1,0:T(8,128)(2,1)} %bitcast.3), calls=%async_computation | async-start | bytes 1048576 | tf_op jit(solution)/shard_map/all_to_all | solution.py:479
  17.9 0.0 copy-done
  17.9 0.1 tile.26
  18.0 0.1 tile.28.a_row
  18.1 0.0 copy-start.1
  18.1 0.1 tile.33.a_col
  18.2 0.6 copy-done.1
  18.7 0.1 tile.30
  18.8 0.0 copy-start.2
  18.8 0.1 tile.34.w_col
  19.0 0.5 copy-done.2
  19.5 0.1 reshape.44.skip
  19.6 4.7 %shard_map.110 = (bf16[1024,512]{1,0:T(8,128)(2,1)}, bf16[2,256,1024]{2,1,0:T(8,128)(2,1)}, f32[1024,256]{1,0:T(8,128)}, f32[1048,128]{1,0:T(8,128)}, bf16[2,256...) custom-call(bf16[32,8192]{1,0:T(8,128)(2,1)} %first_hbm.3, bf16[32,8192]{1,0:T(8,128)(2,1)} %second_hbm.3, ...), custom_call_target="tpu_custom_call" | custom-call | tf_op jit(solution)/shard_map/pallas_call | solution.py:398
  24.3 23.8 %all-to-all-done.grad_out = bf16[64,32,128]{2,1,0:T(8,128)(2,1)S(1)} async-done(((bf16[64,32,128]{2,1,0:T(8,128)(2,1)}), bf16[64,32,128]{2,1,0:T(8,128)(2,1)S(1)}, u32[]{:S(2)}, u32[]{:S(2)}) %all-to-all-start) | async-done | bytes 524320 | tf_op jit(solution)/shard_map/all_to_all | solution.py:479
  48.1 4.2 %shard_map.111 = (f32[8,16,128]{2,1,0:T(8,128)}, bf16[64,32,128]{2,1,0:T(8,128)(2,1)}) custom-call(bf16[64,32,128]{2,1,0:T(8,128)(2,1)S(1)} %all-to-all-done.grad_out, bf16[32,8192]{1,0:T(8,128)(2,1)} %third_hbm.3, bf16[1024,512]{1,0:T(8,128)(2,1)} %get-tuple-element.20.x_cat_hbm, bf16[2,256,1024]{2,1,0:T(8,128)(2,1)} %get-tuple-element.21.x_turn_hbm, ...), custom_call_target="tpu_custom_call" | custom-call | tf_op jit(solution)/shard_map/pallas_call | solution.py:398
  52.3 9.8 %all-to-all-start.1 = ((f32[8,16,128]{2,1,0:T(8,128)}), f32[8,16,128]{2,1,0:T(8,128)S(1)}, u32[]{:S(2)}, u32[]{:S(2)}) async-start(f32[8,16,128]{2,1,0:T(8,128)} %get-tuple-element.23.payload_hbm), calls=%async_computation.1 | async-start | bytes 131072 | tf_op jit(solution)/shard_map/all_to_all | solution.py:485
  62.0 4.0 %shard_map.112 = (f32[1024,256]{1,0:T(8,128)}, f32[17,8,128]{2,1,0:T(8,128)}) custom-call(bf16[64,32,128]{2,1,0:T(8,128)(2,1)} %get-tuple-element.24.grad_out_hbm, bf16[32,8192]{1,0:T(8,128)(2,1)} %third_hbm.3, bf16[2,256,256]{2,1,0:T(8,128)(2,1)} %get-tuple-element.25.back_toep_hbm, bf16[2,128,256]{2,1,0:T(8,128)(2,1)} %get-tuple-element.26.mats_hbm, ...), custom_call_target="tpu_custom_call" | custom-call | tf_op jit(solution)/shard_map/pallas_call | solution.py:398
  66.0 9.9 %all-to-all-done.1.parts = f32[8,16,128]{2,1,0:T(8,128)S(1)} async-done(((f32[8,16,128]{2,1,0:T(8,128)}), f32[8,16,128]{2,1,0:T(8,128)S(1)}, u32[]{:S(2)}, u32[]{:S(2)}) %all-to-all-start.1) | async-done | bytes 65568 | tf_op jit(solution)/shard_map/all_to_all | solution.py:485
  75.9 3.8 %shard_map.113 = (bf16[32,8192]{1,0:T(8,128)(2,1)}, bf16[32,8192]{1,0:T(8,128)(2,1)}, bf16[32,8192]{1,0:T(8,128)(2,1)}, f32[2,16]{1,0:T(2,128)}, f32[1,32]{1,0:T(1,128)}) custom-call(f32[8,16,128]{2,1,0:T(8,128)S(1)} %all-to-all-done.1.parts, f32[17,8,128]{2,1,0:T(8,128)} %get-tuple-element.27.small_hbm, bf16[2,128,256]{2,1,0:T(8,128)(2,1)} %get-tuple-element.26.mats_hbm, ...), custom_call_target="tpu_custom_call" | custom-call | tf_op jit(solution)/shard_map/pallas_call | solution.py:398
  (3 shorter events, 0.0 us)
Async XLA Ops:
  0.6 17.2 %copy-start = (f32[2,16]{1,0:T(2,128)S(1)}, f32[2,16]{1,0:T(2,128)}, u32[]{:S(2)}) copy-start(f32[2,16]{1,0:T(2,128)} %a_s.1) | copy-start | bytes 388
  0.6 47.4 %all-to-all-start = ((bf16[64,32,128]{2,1,0:T(8,128)(2,1)}), bf16[64,32,128]{2,1,0:T(8,128)(2,1)S(1)}, u32[]{:S(2)}, u32[]{:S(2)}) async-start(bf16[64,32,128]{2,1,0:T(8,128)(2,1)} %bitcast.3), calls=%async_computation | async-start | bytes 1048576 | tf_op jit(solution)/shard_map/all_to_all | solution.py:479
  18.1 0.7 copy-start.1
  18.8 0.7 copy-start.2
  52.3 23.7 %all-to-all-start.1 = ((f32[8,16,128]{2,1,0:T(8,128)}), f32[8,16,128]{2,1,0:T(8,128)S(1)}, u32[]{:S(2)}, u32[]{:S(2)}) async-start(f32[8,16,128]{2,1,0:T(8,128)} %get-tuple-element.23.payload_hbm), calls=%async_computation.1 | async-start | bytes 131072 | tf_op jit(solution)/shard_map/all_to_all | solution.py:485

commit v3 on v2

--- a/solution.py
+++ b/solution.py
@@ -136,6 +136,39 @@
     finish(outputs)
 
 
+FIRST = 36
+CH_ORDER = [FIRST if p == 0 else 0 if p == FIRST else p for p in range(SPANS)]
+CTX_ORDER = [5, 1, 3, 7, 2, 0, 4, 6]
+CTX_PLACE = [CTX_ORDER.index(k) for k in range(CTX)]
+RUNS = [(0, 1)] + [(i, min(i + 5, FIRST)) for i in range(1, FIRST, 5)] + [(FIRST, FIRST + 1)]
+RUNS += [(i, min(i + 5, SPANS)) for i in range(FIRST + 1, SPANS, 5)]
+
+
+def swap_copies(source, target, sems, first=0):
+    return begin(
+        [
+            (source.at[pl.ds(CH_ORDER[i], j - i)], target.at[pl.ds(i, j - i)])
+            for i, j in RUNS
+        ],
+        sems,
+        first,
+    )
+
+
+def swap_kernel(heads, swapped, sems):
+    finish(swap_copies(heads, swapped, sems))
+
+
+def swap(heads):
+    return pl.pallas_call(
+        swap_kernel,
+        out_shape=jax.ShapeDtypeStruct(heads.shape, heads.dtype),
+        in_specs=[pl.BlockSpec(memory_space=pltpu.HBM)],
+        out_specs=pl.BlockSpec(memory_space=pltpu.VMEM),
+        scratch_shapes=[pltpu.SemaphoreType.DMA((len(RUNS),))],
+    )(pltpu.with_memory_space_constraint(heads, pltpu.HBM))
+
+
 def middle_kernel(
     grad_out, third_hbm, x_cat_hbm, x_turn_hbm, enter_hbm,
     payload_hbm, grad_out_hbm,
@@ -145,14 +178,14 @@
     enter_in, turn_in, cat_in = begin(
         [(enter_hbm, enter), (x_turn_hbm, x_turn), (x_cat_hbm, x_cat)], sems, 1
     )
-    outputs = begin([(grad_out, grad_out_hbm)], sems, 4)
+    outputs = swap_copies(grad_out, grad_out_hbm, sems, 5)
     row = iota((128, 128), 0)
     col = iota((128, 128), 1)
     token = row.astype(F32)
     finish(early)
     for n in range(SPANS):
         at, here = pl.ds(n * WIDTH, WIDTH), pl.ds(n * SPAN, SPAN)
-        y = grad_out[n].astype(F32) * third[:, here].astype(F32)
+        y = grad_out[CH_ORDER[n]].astype(F32) * third[:, here].astype(F32)
         hi, lo = high(y), low(y)
         for g in range(GROUPS):
             c = slice(g * WIDTH, (g + 1) * WIDTH)
@@ -207,7 +240,7 @@
     for k in range(CTX):
         payload[k, :8, :] = back
         payload[k, 8:, :] = ahead
-    finish(outputs + begin([(payload, payload_hbm)], sems, 5))
+    finish(outputs + begin([(payload, payload_hbm)], sems, 4))
 
 
 def backward_kernel(
@@ -318,7 +351,8 @@
     far = jnp.zeros((8, 128), F32)
     block_step = jnp.exp(-a * float(LENGTH))
     for k in range(CTX):
-        later, earlier = parts[k, :8, :], parts[k, 8:, :]
+        at = CTX_PLACE[k]
+        later, earlier = parts[at, :8, :], parts[at, 8:, :]
         back = back + later * small[k]
         ahead = ahead + earlier * small[CTX + k]
         far = far + later * running
@@ -449,7 +483,7 @@
         middle_kernel,
         [PARTS, ARRIVED],
         [GATE, CAT, TURN, ENTER, CAT, STATES, PARTS],
-        6,
+        5 + len(RUNS),
         (grad_out, third, x_cat, x_turn, enter),
         vmem=(0,),
     )
@@ -477,12 +511,19 @@
 
 def on_device(first, second, third, grad_heads, residue, decay_rate, skip_gain):
     grad_out = lax.all_to_all(
-        grad_heads.reshape(SPANS, GROUPS * WIDTH, SPAN), "ch", split_axis=0, concat_axis=0, tiled=True
+        swap(grad_heads.reshape(SPANS, GROUPS * WIDTH, SPAN)),
+        "ch",
+        split_axis=0,
+        concat_axis=0,
+        tiled=True,
+        axis_index_groups=[CH_ORDER],
     )
     place = lax.axis_index("ctx").astype(jnp.int32).reshape(1)
 
     def exchange(payload):
-        return lax.all_to_all(payload, "ctx", split_axis=0, concat_axis=0, tiled=True)
+        return lax.all_to_all(
+            payload, "ctx", split_axis=0, concat_axis=0, tiled=True, axis_index_groups=[CTX_ORDER]
+        )
 
     return local(first, second, third, grad_out, exchange, residue, decay_rate, skip_gain, place)
 

time: 80.1 us -> 71 us (0.89)
  waiting for transfers between devices: 33.7 us -> 16.8 us
  starting transfers between devices: 27 us -> 32.7 us
  Pallas kernels: 16.7 us -> 18.7 us
    all_to_all x2, waiting for transfers between devices: 33.7 us -> 16.8 us  [the longest x1 16.8 us: on_device(): lax.all_to_all(swap(grad_heads.reshape(SPANS, GROUPS * WIDTH, SPAN)), 'ch...]
    all_to_all x2, starting transfers between devices: 27 us -> 32.7 us  [the longest x1 18.1 us: on_device(): lax.all_to_all(swap(grad_heads.reshape(SPANS, GROUPS * WIDTH, SPAN)), 'ch...]
    pallas_call x0 -> x1, Pallas kernels: none -> 1.94 us  [swap(): pl.pallas_call(swap_kernel, out_shape=jax.ShapeDtypeStruct(heads.shape, h...]
  transfers between devices with their start and end apart: 2 -> 2, of which waited for: 2 -> 1; matrix products, arithmetic and copies ran while one was open for 1% -> 1% of each run, Pallas kernels for 11% -> 12%
where the time goes in v3:
time: 71 us; the launch traced here: 70.6 us
  starting transfers between devices  32.7 us (46%)
  Pallas kernels  18.7 us (26%)
  waiting for transfers between devices  16.8 us (24%)
  local copies, waits for them, and re-layouts  1.68 us (2%)
  between operations  0.72 us (1%)
    all_to_all x1, starting transfers between devices, on_device(): lax.all_to_all(swap(grad_heads.reshape(SPANS, GROUPS * WIDTH, SPAN)), 'ch...  18.1 us
    pallas_call x4, Pallas kernels, call(): pl.pallas_call(kernel, out_shape=tuple((pltpu.HBM(s, d) for s, d in outs)...  16.8 us
    all_to_all x1, waiting for transfers between devices, on_device(): lax.all_to_all(swap(grad_heads.reshape(SPANS, GROUPS * WIDTH, SPAN)), 'ch...  16.8 us
    all_to_all x1, starting transfers between devices, exchange(): lax.all_to_all(payload, 'ctx', split_axis=0, concat_axis=0, tiled=True, a...  14.6 us
    pallas_call x1, Pallas kernels, swap(): pl.pallas_call(swap_kernel, out_shape=jax.ShapeDtypeStruct(heads.shape, h...  1.94 us
  transfers between devices with their start and end apart: 2, of which 1 were waited for; matrix products, arithmetic and copies ran while one was open for 1% of the time, Pallas kernels for 12%

profile of v3, /device:TPU:1, one launch (start us, length us, event | category | flops | bytes accessed | tf_op | source)
XLA Modules:
  0.0 70.6 jit_solution(8688864755214337757)
XLA Ops:
  0.6 1.9 %shard_map.110 = bf16[64,32,128]{2,1,0:T(8,128)(2,1)} custom-call(bf16[64,32,128]{2,1,0:T(8,128)(2,1)} %bitcast.3), custom_call_target="tpu_custom_call" | custom-call | tf_op jit(solution)/shard_map/pallas_call | solution.py:163
  2.6 0.0 copy-start
  2.6 18.1 %all-to-all-start = ((bf16[64,32,128]{2,1,0:T(8,128)(2,1)}), bf16[64,32,128]{2,1,0:T(8,128)(2,1)S(1)}, u32[]{:S(2)}, u32[]{:S(2)}) async-start(bf16[64,32,128]{2,1,0:T(8,128)(2,1)} %shard_map.110), calls=%async_computation | async-start | bytes 1048576 | tf_op jit(solution)/shard_map/all_to_all | solution.py:513
  20.7 0.0 copy-done
  20.7 0.1 tile.26
  20.8 0.1 tile.28.a_row
  20.9 0.0 copy-start.1
  20.9 0.1 tile.33.a_col
  21.0 0.6 copy-done.1
  21.6 0.1 tile.30
  21.7 0.0 copy-start.2
  21.7 0.1 tile.34.w_col
  21.8 0.5 copy-done.2
  22.3 0.1 reshape.44.skip
  22.4 4.7 %shard_map.111 = (bf16[1024,512]{1,0:T(8,128)(2,1)}, bf16[2,256,1024]{2,1,0:T(8,128)(2,1)}, f32[1024,256]{1,0:T(8,128)}, f32[1048,128]{1,0:T(8,128)}, bf16[2,256...) custom-call(bf16[32,8192]{1,0:T(8,128)(2,1)} %first_hbm.3, bf16[32,8192]{1,0:T(8,128)(2,1)} %second_hbm.3, ...), custom_call_target="tpu_custom_call" | custom-call | tf_op jit(solution)/shard_map/pallas_call | solution.py:432
  27.1 16.8 %all-to-all-done.grad_out = bf16[64,32,128]{2,1,0:T(8,128)(2,1)S(1)} async-done(((bf16[64,32,128]{2,1,0:T(8,128)(2,1)}), bf16[64,32,128]{2,1,0:T(8,128)(2,1)S(1)}, u32[]{:S(2)}, u32[]{:S(2)}) %all-to-all-start) | async-done | bytes 524320 | tf_op jit(solution)/shard_map/all_to_all | solution.py:513
  43.9 4.3 %shard_map.112 = (f32[8,16,128]{2,1,0:T(8,128)}, bf16[64,32,128]{2,1,0:T(8,128)(2,1)}) custom-call(bf16[64,32,128]{2,1,0:T(8,128)(2,1)S(1)} %all-to-all-done.grad_out, bf16[32,8192]{1,0:T(8,128)(2,1)} %third_hbm.3, bf16[1024,512]{1,0:T(8,128)(2,1)} %get-tuple-element.20.x_cat_hbm, bf16[2,256,1024]{2,1,0:T(8,128)(2,1)} %get-tuple-element.21.x_turn_hbm, ...), custom_call_target="tpu_custom_call" | custom-call | tf_op jit(solution)/shard_map/pallas_call | solution.py:432
  48.2 14.6 %all-to-all-start.1 = ((f32[8,16,128]{2,1,0:T(8,128)}), f32[8,16,128]{2,1,0:T(8,128)S(1)}, u32[]{:S(2)}, u32[]{:S(2)}) async-start(f32[8,16,128]{2,1,0:T(8,128)} %get-tuple-element.23.payload_hbm), calls=%async_computation.1 | async-start | bytes 131072 | tf_op jit(solution)/shard_map/all_to_all | solution.py:524
  62.8 4.0 %shard_map.113 = (f32[1024,256]{1,0:T(8,128)}, f32[17,8,128]{2,1,0:T(8,128)}) custom-call(bf16[64,32,128]{2,1,0:T(8,128)(2,1)} %get-tuple-element.24.grad_out_hbm, bf16[32,8192]{1,0:T(8,128)(2,1)} %third_hbm.3, bf16[2,256,256]{2,1,0:T(8,128)(2,1)} %get-tuple-element.25.back_toep_hbm, bf16[2,128,256]{2,1,0:T(8,128)(2,1)} %get-tuple-element.26.mats_hbm, ...), custom_call_target="tpu_custom_call" | custom-call | tf_op jit(solution)/shard_map/pallas_call | solution.py:432
  66.8 0.0 all-to-all-done.1.parts
  66.8 3.8 %shard_map.114 = (bf16[32,8192]{1,0:T(8,128)(2,1)}, bf16[32,8192]{1,0:T(8,128)(2,1)}, bf16[32,8192]{1,0:T(8,128)(2,1)}, f32[2,16]{1,0:T(2,128)}, f32[1,32]{1,0:T(1,128)}) custom-call(f32[8,16,128]{2,1,0:T(8,128)S(1)} %all-to-all-done.1.parts, f32[17,8,128]{2,1,0:T(8,128)} %get-tuple-element.27.small_hbm, bf16[2,128,256]{2,1,0:T(8,128)(2,1)} %get-tuple-element.26.mats_hbm, ...), custom_call_target="tpu_custom_call" | custom-call | tf_op jit(solution)/shard_map/pallas_call | solution.py:432
  (3 shorter events, 0.0 us)
Async XLA Ops:
  2.6 18.1 %copy-start = (f32[2,16]{1,0:T(2,128)S(1)}, f32[2,16]{1,0:T(2,128)}, u32[]{:S(2)}) copy-start(f32[2,16]{1,0:T(2,128)} %a_s.1) | copy-start | bytes 388
  2.6 41.3 %all-to-all-start = ((bf16[64,32,128]{2,1,0:T(8,128)(2,1)}), bf16[64,32,128]{2,1,0:T(8,128)(2,1)S(1)}, u32[]{:S(2)}, u32[]{:S(2)}) async-start(bf16[64,32,128]{2,1,0:T(8,128)(2,1)} %shard_map.110), calls=%async_computation | async-start | bytes 1048576 | tf_op jit(solution)/shard_map/all_to_all | solution.py:513
  20.9 0.7 copy-start.1
  21.7 0.7 copy-start.2
  48.2 18.5 %all-to-all-start.1 = ((f32[8,16,128]{2,1,0:T(8,128)}), f32[8,16,128]{2,1,0:T(8,128)S(1)}, u32[]{:S(2)}, u32[]{:S(2)}) async-start(f32[8,16,128]{2,1,0:T(8,128)} %get-tuple-element.23.payload_hbm), calls=%async_computation.1 | async-start | bytes 131072 | tf_op jit(solution)/shard_map/all_to_all | solution.py:524

commit v4 on v3

--- a/solution.py
+++ b/solution.py
@@ -86,11 +86,12 @@
 
 
 def forward_kernel(
-    first_hbm, second_hbm, a_row, a_col, w_col, a_s, w_s, skip,
-    x_cat_hbm, x_turn_hbm, conv_hbm, enter_hbm, back_toep_hbm, mats_hbm,
-    first, second, x_cat, x_turn, conv, enter, back_toep, mats, states, toep, sems,
+    first_hbm, second_hbm, third_hbm, a_row, a_col, w_col, a_s, w_s, skip,
+    x_turn, enter, edge, third, x_cat_hbm, conv_hbm, back_toep_hbm, mats_hbm,
+    first, second, x_cat, conv, back_toep, mats, states, toep, sems,
 ):
     inputs = begin([(first_hbm, first), (second_hbm, second)], sems)
+    outputs = begin([(third_hbm, third)], sems, 6)
     a = a_row[...]
     row = iota((128, 128), 0)
     col = iota((128, 128), 1)
@@ -101,7 +102,7 @@
     for g in range(GROUPS):
         toep[g] = toeplitz(a_s, w_s, g, col - row)
         back_toep[g] = toeplitz(a_s, w_s, g, row - col)
-    outputs = begin([(back_toep, back_toep_hbm), (mats, mats_hbm)], sems, 2)
+    outputs += begin([(back_toep, back_toep_hbm), (mats, mats_hbm)], sems, 2)
     finish(inputs)
     for n in range(SPANS):
         at, here = pl.ds(n * WIDTH, WIDTH), pl.ds(n * SPAN, SPAN)
@@ -115,15 +116,14 @@
     states[...] = halves(dot(x_cat[...], state_matrix(a, 128.0 - token)))
     step = jnp.exp(-a * 128.0)
     carry = jnp.zeros((WIDTH, 128), F32)
+    lane = iota((WIDTH, 128), 1)
     for n in range(SPANS):
         at = pl.ds(n * WIDTH, WIDTH)
-        enter[at, :] = carry
+        enter[at, :] = quad_split(carry, lane)
         carry = carry * step + states[at, :]
-    enter[pl.ds(ROWS, WIDTH), :] = carry
-    enter[pl.ds(ROWS + WIDTH, 8), :] = jnp.broadcast_to(a, (8, 128))
-    outputs += begin([(enter, enter_hbm)], sems, 5)
-    lane = iota((ROWS, 128), 1)
-    conv[...] = dot(quad_split(enter[pl.ds(0, ROWS), :], lane), mats[0])
+    edge[:WIDTH, :] = carry
+    edge[WIDTH:, :] = jnp.broadcast_to(a, (8, 128))
+    conv[...] = dot(enter[...], mats[0])
     for g in range(GROUPS):
         mine = pl.ds(256 * g, 256)
         here = pl.ds(128 * g, 128)
@@ -132,7 +132,7 @@
         gated = x[:, :128].astype(F32) + x[:, 128:].astype(F32)
         conv[:, here] = conv[:, here] + halves(dot(x, toep[g])) + gain * gated
         x_turn[g] = x.T
-    outputs += begin([(x_turn, x_turn_hbm), (conv, conv_hbm)], sems, 6)
+    outputs += begin([(conv, conv_hbm)], sems, 5)
     finish(outputs)
 
 
@@ -162,7 +162,7 @@
 def swap(heads):
     return pl.pallas_call(
         swap_kernel,
-        out_shape=jax.ShapeDtypeStruct(heads.shape, heads.dtype),
+        out_shape=pltpu.VMEM(heads.shape, heads.dtype),
         in_specs=[pl.BlockSpec(memory_space=pltpu.HBM)],
         out_specs=pl.BlockSpec(memory_space=pltpu.VMEM),
         scratch_shapes=[pltpu.SemaphoreType.DMA((len(RUNS),))],
@@ -170,19 +170,14 @@
 
 
 def middle_kernel(
-    grad_out, third_hbm, x_cat_hbm, x_turn_hbm, enter_hbm,
-    payload_hbm, grad_out_hbm,
-    third, x_cat, x_turn, enter, g_cat, states, payload, sems,
+    grad_out, third, x_turn, enter, edge, x_cat_hbm,
+    payload,
+    x_cat, g_cat, states, sems,
 ):
-    early = begin([(third_hbm, third)], sems)
-    enter_in, turn_in, cat_in = begin(
-        [(enter_hbm, enter), (x_turn_hbm, x_turn), (x_cat_hbm, x_cat)], sems, 1
-    )
-    outputs = swap_copies(grad_out, grad_out_hbm, sems, 5)
+    cat_in = begin([(x_cat_hbm, x_cat)], sems)
     row = iota((128, 128), 0)
     col = iota((128, 128), 1)
     token = row.astype(F32)
-    finish(early)
     for n in range(SPANS):
         at, here = pl.ds(n * WIDTH, WIDTH), pl.ds(n * SPAN, SPAN)
         y = grad_out[CH_ORDER[n]].astype(F32) * third[:, here].astype(F32)
@@ -191,10 +186,8 @@
             c = slice(g * WIDTH, (g + 1) * WIDTH)
             g_cat[at, pl.ds(256 * g, 128)] = hi[c]
             g_cat[at, pl.ds(256 * g + 128, 128)] = lo[c]
-    finish([enter_in])
-    a = enter[pl.ds(ROWS + WIDTH, 1), :]
+    a = edge[WIDTH : WIDTH + 1, :]
     states[...] = halves(dot(g_cat[...], state_matrix(a, token + 1.0)))
-    finish([turn_in])
     cross = []
     for g in range(GROUPS):
         four = dot(x_turn[g], g_cat[:, pl.ds(256 * g, 256)])
@@ -210,10 +203,11 @@
     for n in reversed(range(SPANS)):
         at = pl.ds(n * WIDTH, WIDTH)
         now = states[at, :]
-        far = far + now * enter[at, :]
+        far = far + now * enter[at, :].astype(F32)
         carry = carry * step + now
-    weight = near + (far[:8] + far[8:]) * jnp.exp(a)
-    finish([cat_in])
+    far = far[:8] + far[8:]
+    weight = near + (far + pltpu.roll(far, 32, 1)) * jnp.exp(a)
+    finish(cat_in)
     total = []
     for g in range(GROUPS):
         mine = jnp.zeros((WIDTH, SPAN), F32)
@@ -235,21 +229,19 @@
     back = jnp.where(
         quarter == 0, carry[:8], jnp.where(quarter == 1, carry[8:], jnp.where(quarter == 2, weight, direct))
     )
-    state = enter[pl.ds(ROWS, WIDTH), :]
-    ahead = jnp.where(quarter == 0, state[:8, :], state[8:, :])
+    ahead = jnp.where(quarter == 0, edge[0:8, :], edge[8:16, :])
     for k in range(CTX):
         payload[k, :8, :] = back
         payload[k, 8:, :] = ahead
-    finish(outputs + begin([(payload, payload_hbm)], sems, 4))
 
 
 def backward_kernel(
-    grad_out_hbm, third_hbm, back_toep_hbm, mats_hbm, a_row, skip, place, payload_hbm,
-    mixed_hbm, small_hbm,
-    grad_out, third, back_toep, mats, g_cat, states, leave, mixed, small, sems,
+    grad_out, third, back_toep_hbm, mats_hbm, conv_hbm, a_row, skip, place, payload,
+    mixed, small, mats, conv,
+    back_toep, g_cat, states, leave, sems,
 ):
-    early = begin(
-        [(grad_out_hbm, grad_out), (third_hbm, third), (back_toep_hbm, back_toep), (mats_hbm, mats)], sems
+    mats_in, toep_in, conv_in = begin(
+        [(mats_hbm, mats), (back_toep_hbm, back_toep), (conv_hbm, conv)], sems
     )
     a = a_row[...]
     token = iota((128, 128), 0).astype(F32)
@@ -264,11 +256,9 @@
         small[k] = jnp.where(is_state, jnp.exp(-wide * after) * later, 1.0)
         small[CTX + k] = jnp.exp(-wide * before) * earlier
     small[2 * CTX] = jnp.broadcast_to(a, (8, 128))
-    outputs = begin([(small, small_hbm)], sems, 4)
-    finish(early)
     for n in range(SPANS):
         at, here = pl.ds(n * WIDTH, WIDTH), pl.ds(n * SPAN, SPAN)
-        y = grad_out[n].astype(F32) * third[:, here].astype(F32)
+        y = grad_out[CH_ORDER[n]].astype(F32) * third[:, here].astype(F32)
         hi, lo = high(y), low(y)
         for g in range(GROUPS):
             c = slice(g * WIDTH, (g + 1) * WIDTH)
@@ -282,15 +272,16 @@
         leave[at, :] = carry
         carry = carry * step + states[at, :]
     lane = iota((ROWS, 128), 1)
+    finish([mats_in])
     mixed[...] = dot(quad_split(leave[...], lane), mats[1])
+    finish([toep_in])
     for g in range(GROUPS):
         here = pl.ds(128 * g, 128)
         y = g_cat[:, pl.ds(256 * g, 256)]
         gain = jnp.concatenate([skip[g]] * SPANS, axis=0)
         grad_conv = y[:, :128].astype(F32) + y[:, 128:].astype(F32)
         mixed[:, here] = mixed[:, here] + halves(dot(y, back_toep[g])) + gain * grad_conv
-    outputs += begin([(mixed, mixed_hbm)], sems, 5)
-    finish(outputs)
+    finish([conv_in])
 
 
 CHUNKS = 4
@@ -300,9 +291,9 @@
 
 
 def finish_kernel(
-    parts, small_hbm, mats_hbm, conv_hbm, mixed_hbm, grad_out_hbm, first_hbm, second_hbm,
+    parts, small, mats, conv, mixed, grad_out, first_hbm, second_hbm,
     grad_first_hbm, grad_second_hbm, grad_third_hbm, grad_residue_hbm, grad_skip_hbm,
-    small, mats, conv, mixed, grad_out, first, second, grad_first, grad_second, grad_third, grad_residue, grad_skip, decays,
+    first, second, grad_first, grad_second, grad_third, grad_residue, grad_skip, decays,
     sems,
 ):
     def rows_of(c):
@@ -314,35 +305,19 @@
     def tokens_of(c):
         return pl.ds(c * CHUNK_TOKENS, CHUNK_TOKENS)
 
-    early = begin([(small_hbm, small), (mats_hbm, mats)], sems)
-    used = 2
-    third_in, gate_in = [], []
-    for c in range(CHUNKS):
-        third_in.append(
-            begin(
-                [
-                    (conv_hbm.at[rows_of(c), :], conv.at[rows_of(c), :]),
-                    (grad_out_hbm.at[spans_of(c)], grad_out.at[spans_of(c)]),
-                ],
-                sems,
-                used,
-            )
-        )
-        used += 2
+    gate_in = []
     for c in range(CHUNKS):
         gate_in.append(
             begin(
                 [
-                    (mixed_hbm.at[rows_of(c), :], mixed.at[rows_of(c), :]),
                     (first_hbm.at[:, tokens_of(c)], first.at[:, tokens_of(c)]),
                     (second_hbm.at[:, tokens_of(c)], second.at[:, tokens_of(c)]),
                 ],
                 sems,
-                used,
+                2 * c,
             )
         )
-        used += 3
-    finish(early)
+    used = 2 * CHUNKS
     a = small[2 * CTX, 0:1, :]
     quarter = iota((8, 128), 1) // 32
     back = jnp.zeros((8, 128), F32)
@@ -384,11 +359,10 @@
     entering, leaving = rows(ahead), rows(back)
     for c in range(CHUNKS):
         add = fix(entering, 0, c)
-        finish(third_in[c])
         full = conv[rows_of(c), :] + add
         for i in range(CHUNK_SPANS):
             n = c * CHUNK_SPANS + i
-            grad_third[:, pl.ds(n * SPAN, SPAN)] = (grad_out[n].astype(F32) * channels(full, i)).astype(BF16)
+            grad_third[:, pl.ds(n * SPAN, SPAN)] = (grad_out[CH_ORDER[n]].astype(F32) * channels(full, i)).astype(BF16)
         outputs += begin([(grad_third.at[:, tokens_of(c)], grad_third_hbm.at[:, tokens_of(c)])], sems, used)
         used += 1
     near = spread(back, 2)
@@ -422,26 +396,33 @@
     finish(outputs)
 
 
-FINISH_COPIES = 2 + 5 * CHUNKS + 3 * CHUNKS + 2
-
-
-def call(kernel, outs, scratch, copies, args, vmem=(), smem=()):
+FINISH_COPIES = 2 * CHUNKS + 3 * CHUNKS + 2
+
+
+def placed(kind, shape, dtype):
+    return kind(shape, dtype)
+
+
+def pin(x, kind):
+    return pltpu.with_memory_space_constraint(x, kind)
+
+
+def call(kernel, outs, scratch, copies, args, near=(), vmem=(), smem=(), outs_near=()):
     def space(i):
-        return pltpu.VMEM if i in vmem else pltpu.SMEM if i in smem else pltpu.HBM
-
+        return pltpu.VMEM if i in vmem or i in near else pltpu.SMEM if i in smem else pltpu.HBM
+
+    def pinned(i, x):
+        return x if i in vmem or i in smem else pin(x, space(i))
+
+    kinds = [pltpu.VMEM if i in outs_near else pltpu.HBM for i in range(len(outs))]
     return pl.pallas_call(
         kernel,
-        out_shape=tuple(pltpu.HBM(s, d) for s, d in outs),
+        out_shape=tuple(placed(kind, s, d) for kind, (s, d) in zip(kinds, outs)),
         in_specs=[pl.BlockSpec(memory_space=space(i)) for i in range(len(args))],
-        out_specs=tuple(pl.BlockSpec(memory_space=pltpu.HBM) for _ in outs),
+        out_specs=tuple(pl.BlockSpec(memory_space=kind) for kind in kinds),
         scratch_shapes=[pltpu.VMEM(s, d) for s, d in scratch] + [pltpu.SemaphoreType.DMA((copies,))],
         compiler_params=pltpu.CompilerParams(vmem_limit_bytes=40 << 20),
-    )(
-        *(
-            pltpu.with_memory_space_constraint(x, pltpu.HBM) if space(i) == pltpu.HBM else x
-            for i, x in enumerate(args)
-        )
-    )
+    )(*(pinned(i, x) for i, x in enumerate(args)))
 
 
 def prepare(residue, decay_rate, skip_gain):
@@ -458,7 +439,8 @@
 TURN = ((GROUPS, 256, ROWS), BF16)
 WHOLE = ((ROWS, 256), F32)
 STATES = ((ROWS, 128), F32)
-ENTER = ((ROWS + WIDTH + 8, 128), F32)
+ENTER = ((ROWS, 128), BF16)
+EDGE = ((WIDTH + 8, 128), F32)
 TOEP = ((GROUPS, 256, 256), BF16)
 MATS = ((2, 128, 256), BF16)
 PARTS = ((CTX, 16, 128), F32)
@@ -469,42 +451,45 @@
 
 def local(first, second, third, grad_out, exchange, residue, decay_rate, skip_gain, place):
     a_row, a_col, w_col, weight, skip = prepare(residue, decay_rate, skip_gain)
-    outs = [CAT, TURN, WHOLE, ENTER, TOEP, MATS]
-    x_cat, x_turn, conv, enter, back_toep, mats = call(
+    x_turn, enter, edge, third, x_cat, conv, back_toep, mats = call(
         forward_kernel,
-        outs,
-        [GATE, GATE] + outs + [STATES, TOEP],
-        8,
-        (first, second, a_row, a_col, w_col, decay_rate, weight, skip),
-        vmem=(2, 3, 4, 7),
-        smem=(5, 6),
-    )
-    payload, grad_out = call(
+        [TURN, ENTER, EDGE, GATE, CAT, WHOLE, TOEP, MATS],
+        [GATE, GATE, CAT, WHOLE, TOEP, MATS, STATES, TOEP],
+        7,
+        (first, second, third, a_row, a_col, w_col, decay_rate, weight, skip),
+        vmem=(3, 4, 5, 8),
+        smem=(6, 7),
+        outs_near=(0, 1, 2, 3),
+    )
+    (payload,) = call(
         middle_kernel,
-        [PARTS, ARRIVED],
-        [GATE, CAT, TURN, ENTER, CAT, STATES, PARTS],
-        5 + len(RUNS),
-        (grad_out, third, x_cat, x_turn, enter),
-        vmem=(0,),
+        [PARTS],
+        [CAT, CAT, STATES],
+        1,
+        (grad_out, third, x_turn, enter, edge, x_cat),
+        near=(0, 1, 2, 3, 4),
+        outs_near=(0,),
     )
     parts = exchange(payload)
-    mixed, small = call(
+    mixed, small, mats, conv = call(
         backward_kernel,
-        [WHOLE, SMALL],
-        [ARRIVED, GATE, TOEP, MATS, CAT, STATES, STATES, WHOLE, SMALL],
-        6,
-        (grad_out, third, back_toep, mats, a_row, skip, place, payload),
-        vmem=(4, 5),
-        smem=(6,),
+        [WHOLE, SMALL, MATS, WHOLE],
+        [TOEP, CAT, STATES, STATES],
+        3,
+        (grad_out, third, back_toep, mats, conv, a_row, skip, place, payload),
+        near=(0, 1, 8),
+        vmem=(5, 6),
+        smem=(7,),
+        outs_near=(0, 1, 2, 3),
     )
     outs = [GATE, GATE, GATE, RESIDUE, SKIP]
     grad_first, grad_second, grad_third, grad_residue, grad_skip = call(
         finish_kernel,
         outs,
-        [SMALL, MATS, WHOLE, WHOLE, ARRIVED, GATE, GATE] + outs + [((2, SPANS, 128), F32)],
+        [GATE, GATE] + outs + [((2, SPANS, 128), F32)],
         FINISH_COPIES,
         (parts, small, mats, conv, mixed, grad_out, first, second),
-        vmem=(0,),
+        near=(0, 1, 2, 3, 4, 5),
     )
     return grad_first, grad_second, grad_third, grad_residue, grad_skip.reshape(GROUPS * WIDTH)
 

time: 71 us -> 66.9 us (0.942)
  Pallas kernels: 18.7 us -> 14.4 us
    pallas_call x5, Pallas kernels: 18.7 us -> 14.4 us  [the longest x4 12.4 us: call(): pl.pallas_call(kernel, out_shape=tuple((placed(kind, s, d) for kind, (s,...]
  transfers between devices with their start and end apart: 2 -> 2, of which waited for: 1 -> 1; matrix products, arithmetic and copies ran while one was open for 1% -> 1% of each run, Pallas kernels for 12% -> 11%
where the time goes in v4:
time: 66.9 us; the launch traced here: 66.4 us
  starting transfers between devices  32.7 us (49%)
  waiting for transfers between devices  16.9 us (25%)
  Pallas kernels  14.4 us (22%)
  local copies, waits for them, and re-layouts  1.68 us (3%)
  between operations  0.72 us (1%)
    all_to_all x1, starting transfers between devices, on_device(): lax.all_to_all(swap(grad_heads.reshape(SPANS, GROUPS * WIDTH, SPAN)), 'ch...  18.1 us
    all_to_all x1, waiting for transfers between devices, on_device(): lax.all_to_all(swap(grad_heads.reshape(SPANS, GROUPS * WIDTH, SPAN)), 'ch...  16.9 us
    all_to_all x1, starting transfers between devices, exchange(): lax.all_to_all(payload, 'ctx', split_axis=0, concat_axis=0, tiled=True, a...  14.6 us
    pallas_call x4, Pallas kernels, call(): pl.pallas_call(kernel, out_shape=tuple((placed(kind, s, d) for kind, (s,...  12.4 us
    pallas_call x1, Pallas kernels, swap(): pl.pallas_call(swap_kernel, out_shape=pltpu.VMEM(heads.shape, heads.dtype...  1.94 us
  transfers between devices with their start and end apart: 2, of which 1 were waited for; matrix products, arithmetic and copies ran while one was open for 1% of the time, Pallas kernels for 11%

profile of v4, /device:TPU:1, one launch (start us, length us, event | category | flops | bytes accessed | tf_op | source)
XLA Modules:
  0.0 66.4 jit_solution(12132636189475265577)
XLA Ops:
  0.6 1.9 %shard_map.110 = bf16[64,32,128]{2,1,0:T(8,128)(2,1)} custom-call(bf16[64,32,128]{2,1,0:T(8,128)(2,1)} %bitcast.3), custom_call_target="tpu_custom_call" | custom-call | tf_op jit(solution)/shard_map/pallas_call | solution.py:163
  2.6 0.0 copy-start
  2.6 18.1 %all-to-all-start = ((bf16[64,32,128]{2,1,0:T(8,128)(2,1)}), bf16[64,32,128]{2,1,0:T(8,128)(2,1)S(1)}, u32[]{:S(2)}, u32[]{:S(2)}) async-start(bf16[64,32,128]{2,1,0:T(8,128)(2,1)} %shard_map.110), calls=%async_computation | async-start | bytes 1048576 | tf_op jit(solution)/shard_map/all_to_all | solution.py:498
  20.7 0.0 copy-done
  20.7 0.1 tile.26
  20.8 0.1 tile.28.a_row
  20.9 0.0 copy-start.1
  20.9 0.1 tile.33.a_col
  21.0 0.6 copy-done.1
  21.6 0.1 tile.30
  21.7 0.0 copy-start.2
  21.7 0.1 tile.34.w_col
  21.8 0.5 copy-done.2
  22.3 0.1 reshape.44.skip
  22.4 4.6 %shard_map.111 = (bf16[2,256,1024]{2,1,0:T(8,128)(2,1)S(1)}, bf16[1024,128]{1,0:T(8,128)(2,1)S(1)}, f32[24,128]{1,0:T(8,128)S(1)}, bf16[32,8192]{1,0:T(8,128)(2,...) custom-call(bf16[32,8192]{1,0:T(8,128)(2,1)} %first_hbm.3, ...), custom_call_target="tpu_custom_call" | custom-call | tf_op jit(solution)/shard_map/pallas_call | solution.py:418
  27.0 16.9 %all-to-all-done.grad_out = bf16[64,32,128]{2,1,0:T(8,128)(2,1)S(1)} async-done(((bf16[64,32,128]{2,1,0:T(8,128)(2,1)}), bf16[64,32,128]{2,1,0:T(8,128)(2,1)S(1)}, u32[]{:S(2)}, u32[]{:S(2)}) %all-to-all-start) | async-done | bytes 524320 | tf_op jit(solution)/shard_map/all_to_all | solution.py:498
  43.9 2.5 %shard_map.112.payload = f32[8,16,128]{2,1,0:T(8,128)} custom-call(bf16[64,32,128]{2,1,0:T(8,128)(2,1)S(1)} %all-to-all-done.grad_out, bf16[32,8192]{1,0:T(8,128)(2,1)S(1)} %get-tuple-element.22.third, bf16[2,256,1024]{2,1,0:T(8,128)(2,1)S(1)} %get-tuple-element.23.x_turn, bf16[1024,128]{1,0:T(8,128)(2,1)S(1)} %get-tuple-element.24.enter, ...), custom_call_target="tpu_custom_call" | custom-call | tf_op jit(solution)/shard_map/pallas_call | solution.py:418
  46.4 14.6 %all-to-all-start.1 = ((f32[8,16,128]{2,1,0:T(8,128)}), f32[8,16,128]{2,1,0:T(8,128)S(1)}, u32[]{:S(2)}, u32[]{:S(2)}) async-start(f32[8,16,128]{2,1,0:T(8,128)} %shard_map.112.payload), calls=%async_computation.1 | async-start | bytes 131072 | tf_op jit(solution)/shard_map/all_to_all | solution.py:509
  60.9 2.8 %shard_map.113 = (f32[1024,256]{1,0:T(8,128)S(1)}, f32[17,8,128]{2,1,0:T(8,128)S(1)}, bf16[2,128,256]{2,1,0:T(8,128)(2,1)S(1)}, f32[1024,256]{1,0:T(8,128)S(1)}) custom-call(bf16[64,32,128]{2,1,0:T(8,128)(2,1)S(1)} %all-to-all-done.grad_out, bf16[32,8192]{1,0:T(8,128)(2,1)S(1)} %get-tuple-element.22.third, ...), custom_call_target="tpu_custom_call" | custom-call | tf_op jit(solution)/shard_map/pallas_call | solution.py:418
  63.8 0.0 all-to-all-done.1.parts
  63.8 2.6 %shard_map.114 = (bf16[32,8192]{1,0:T(8,128)(2,1)}, bf16[32,8192]{1,0:T(8,128)(2,1)}, bf16[32,8192]{1,0:T(8,128)(2,1)}, f32[2,16]{1,0:T(2,128)}, f32[1,32]{1,0:T(1,128)}) custom-call(f32[8,16,128]{2,1,0:T(8,128)S(1)} %all-to-all-done.1.parts, f32[17,8,128]{2,1,0:T(8,128)S(1)} %get-tuple-element.30.small, bf16[2,128,256]{2,1,0:T(8,128)(2,1)S(1)} %get-tuple-element.31.mats, ...), custom_call_target="tpu_custom_call" | custom-call | tf_op jit(solution)/shard_map/pallas_call | solution.py:418
  (3 shorter events, 0.0 us)
Async XLA Ops:
  2.6 18.1 %copy-start = (f32[2,16]{1,0:T(2,128)S(1)}, f32[2,16]{1,0:T(2,128)}, u32[]{:S(2)}) copy-start(f32[2,16]{1,0:T(2,128)} %a_s.1) | copy-start | bytes 388
  2.6 41.3 %all-to-all-start = ((bf16[64,32,128]{2,1,0:T(8,128)(2,1)}), bf16[64,32,128]{2,1,0:T(8,128)(2,1)S(1)}, u32[]{:S(2)}, u32[]{:S(2)}) async-start(bf16[64,32,128]{2,1,0:T(8,128)(2,1)} %shard_map.110), calls=%async_computation | async-start | bytes 1048576 | tf_op jit(solution)/shard_map/all_to_all | solution.py:498
  20.9 0.7 %copy-start.1 = (f32[2,16]{1,0:T(2,128)S(1)}, f32[2,16]{1,0:T(2,128)}, u32[]{:S(2)}) copy-start(f32[2,16]{1,0:T(2,128)} %param.11) | copy-start | bytes 388
  21.7 0.7 copy-start.2
  46.4 17.4 %all-to-all-start.1 = ((f32[8,16,128]{2,1,0:T(8,128)}), f32[8,16,128]{2,1,0:T(8,128)S(1)}, u32[]{:S(2)}, u32[]{:S(2)}) async-start(f32[8,16,128]{2,1,0:T(8,128)} %shard_map.112.payload), calls=%async_computation.1 | async-start | bytes 131072 | tf_op jit(solution)/shard_map/all_to_all | solution.py:509

commit v5 on v4

--- a/solution.py
+++ b/solution.py
@@ -87,11 +87,11 @@
 
 def forward_kernel(
     first_hbm, second_hbm, third_hbm, a_row, a_col, w_col, a_s, w_s, skip,
-    x_turn, enter, edge, third, x_cat_hbm, conv_hbm, back_toep_hbm, mats_hbm,
-    first, second, x_cat, conv, back_toep, mats, states, toep, sems,
+    x_turn, edge, third, gated, pairs, conv_hbm, back_toep_hbm, mats_hbm,
+    first, second, x_cat, enter, conv, back_toep, mats, states, toep, sems,
 ):
     inputs = begin([(first_hbm, first), (second_hbm, second)], sems)
-    outputs = begin([(third_hbm, third)], sems, 6)
+    outputs = begin([(third_hbm, third)], sems, 5)
     a = a_row[...]
     row = iota((128, 128), 0)
     col = iota((128, 128), 1)
@@ -110,9 +110,9 @@
         hi, lo = high(x), low(x)
         for g in range(GROUPS):
             c = slice(g * WIDTH, (g + 1) * WIDTH)
+            gated[at, pl.ds(128 * g, 128)] = x[c]
             x_cat[at, pl.ds(256 * g, 128)] = hi[c]
             x_cat[at, pl.ds(256 * g + 128, 128)] = lo[c]
-    outputs += begin([(x_cat, x_cat_hbm)], sems, 4)
     states[...] = halves(dot(x_cat[...], state_matrix(a, 128.0 - token)))
     step = jnp.exp(-a * 128.0)
     carry = jnp.zeros((WIDTH, 128), F32)
@@ -123,61 +123,58 @@
         carry = carry * step + states[at, :]
     edge[:WIDTH, :] = carry
     edge[WIDTH:, :] = jnp.broadcast_to(a, (8, 128))
+    odd = iota((WIDTH, 128), 1) >= 64
+    for n in range(0, SPANS, 2):
+        even_rows, odd_rows = enter[pl.ds(n * WIDTH, WIDTH), :], enter[pl.ds((n + 1) * WIDTH, WIDTH), :]
+        pairs[pl.ds(n * WIDTH // 2, WIDTH), :] = jnp.where(
+            odd, odd_rows.astype(F32), even_rows.astype(F32)
+        ).astype(BF16)
     conv[...] = dot(enter[...], mats[0])
     for g in range(GROUPS):
         mine = pl.ds(256 * g, 256)
         here = pl.ds(128 * g, 128)
         x = x_cat[:, mine]
         gain = jnp.concatenate([skip[g]] * SPANS, axis=0)
-        gated = x[:, :128].astype(F32) + x[:, 128:].astype(F32)
-        conv[:, here] = conv[:, here] + halves(dot(x, toep[g])) + gain * gated
+        conv[:, here] = conv[:, here] + halves(dot(x, toep[g])) + gain * gated[:, here]
         x_turn[g] = x.T
-    outputs += begin([(conv, conv_hbm)], sems, 5)
+    outputs += begin([(conv, conv_hbm)], sems, 4)
     finish(outputs)
 
 
-FIRST = 36
+FIRST = 45
 CH_ORDER = [FIRST if p == 0 else 0 if p == FIRST else p for p in range(SPANS)]
 CTX_ORDER = [5, 1, 3, 7, 2, 0, 4, 6]
 CTX_PLACE = [CTX_ORDER.index(k) for k in range(CTX)]
-RUNS = [(0, 1)] + [(i, min(i + 5, FIRST)) for i in range(1, FIRST, 5)] + [(FIRST, FIRST + 1)]
-RUNS += [(i, min(i + 5, SPANS)) for i in range(FIRST + 1, SPANS, 5)]
-
-
-def swap_copies(source, target, sems, first=0):
-    return begin(
-        [
-            (source.at[pl.ds(CH_ORDER[i], j - i)], target.at[pl.ds(i, j - i)])
-            for i, j in RUNS
-        ],
-        sems,
-        first,
-    )
-
-
-def swap_kernel(heads, swapped, sems):
-    finish(swap_copies(heads, swapped, sems))
+RUNS = [(0, 1), (FIRST, FIRST + 1)]
+RUNS += [(i, min(i + 9, FIRST)) for i in range(1, FIRST, 9)]
+RUNS += [(i, min(i + 9, SPANS)) for i in range(FIRST + 1, SPANS, 9)]
+
+
+def swap_kernel(heads, swapped, held, sems):
+    arriving = begin(
+        [(heads.at[pl.ds(CH_ORDER[i], j - i)], held.at[pl.ds(i, j - i)]) for i, j in RUNS], sems
+    )
+    leaving = []
+    for r, (i, j) in enumerate(RUNS):
+        finish([arriving[r]])
+        leaving += begin([(held.at[pl.ds(i, j - i)], swapped.at[pl.ds(i, j - i)])], sems, len(RUNS) + r)
+    finish(leaving)
 
 
 def swap(heads):
-    return pl.pallas_call(
-        swap_kernel,
-        out_shape=pltpu.VMEM(heads.shape, heads.dtype),
-        in_specs=[pl.BlockSpec(memory_space=pltpu.HBM)],
-        out_specs=pl.BlockSpec(memory_space=pltpu.VMEM),
-        scratch_shapes=[pltpu.SemaphoreType.DMA((len(RUNS),))],
-    )(pltpu.with_memory_space_constraint(heads, pltpu.HBM))
+    (swapped,) = call(swap_kernel, [ARRIVED], [ARRIVED], 2 * len(RUNS), (heads,))
+    return swapped
 
 
 def middle_kernel(
-    grad_out, third, x_turn, enter, edge, x_cat_hbm,
-    payload,
-    x_cat, g_cat, states, sems,
+    grad_out, third, x_turn, edge, gated, pairs,
+    payload, states_hbm,
+    g_cat, states, sems,
 ):
-    cat_in = begin([(x_cat_hbm, x_cat)], sems)
     row = iota((128, 128), 0)
     col = iota((128, 128), 1)
     token = row.astype(F32)
+    total = [jnp.zeros((WIDTH, SPAN), F32) for _ in range(GROUPS)]
     for n in range(SPANS):
         at, here = pl.ds(n * WIDTH, WIDTH), pl.ds(n * SPAN, SPAN)
         y = grad_out[CH_ORDER[n]].astype(F32) * third[:, here].astype(F32)
@@ -186,8 +183,10 @@
             c = slice(g * WIDTH, (g + 1) * WIDTH)
             g_cat[at, pl.ds(256 * g, 128)] = hi[c]
             g_cat[at, pl.ds(256 * g + 128, 128)] = lo[c]
+            total[g] = total[g] + y[c] * gated[at, pl.ds(128 * g, 128)]
     a = edge[WIDTH : WIDTH + 1, :]
     states[...] = halves(dot(g_cat[...], state_matrix(a, token + 1.0)))
+    outputs = begin([(states, states_hbm)], sems)
     cross = []
     for g in range(GROUPS):
         four = dot(x_turn[g], g_cat[:, pl.ds(256 * g, 256)])
@@ -200,24 +199,14 @@
     step = jnp.exp(-a * 128.0)
     carry = jnp.zeros((WIDTH, 128), F32)
     far = jnp.zeros((WIDTH, 128), F32)
-    for n in reversed(range(SPANS)):
-        at = pl.ds(n * WIDTH, WIDTH)
-        now = states[at, :]
-        far = far + now * enter[at, :].astype(F32)
-        carry = carry * step + now
+    odd = iota((WIDTH, 128), 1) >= 64
+    for n in reversed(range(0, SPANS, 2)):
+        later, earlier = states[pl.ds((n + 1) * WIDTH, WIDTH), :], states[pl.ds(n * WIDTH, WIDTH), :]
+        far = far + jnp.where(odd, later, earlier) * pairs[pl.ds(n * WIDTH // 2, WIDTH), :].astype(F32)
+        carry = (carry * step + later) * step + earlier
     far = far[:8] + far[8:]
-    weight = near + (far + pltpu.roll(far, 32, 1)) * jnp.exp(a)
-    finish(cat_in)
-    total = []
-    for g in range(GROUPS):
-        mine = jnp.zeros((WIDTH, SPAN), F32)
-        hi, lo = pl.ds(256 * g, 128), pl.ds(256 * g + 128, 128)
-        for n in range(SPANS):
-            at = pl.ds(n * WIDTH, WIDTH)
-            x = x_cat[at, hi].astype(F32) + x_cat[at, lo].astype(F32)
-            y = g_cat[at, hi].astype(F32) + g_cat[at, lo].astype(F32)
-            mine = mine + x * y
-        total.append(mine)
+    far = far + pltpu.roll(far, 32, 1)
+    weight = near + (far + pltpu.roll(far, 64, 1)) * jnp.exp(a)
     direct = lax.dot_general(
         jnp.ones((8, SPAN), F32),
         jnp.concatenate(total * 4, axis=0),
@@ -233,18 +222,18 @@
     for k in range(CTX):
         payload[k, :8, :] = back
         payload[k, 8:, :] = ahead
+    finish(outputs)
 
 
 def backward_kernel(
-    grad_out, third, back_toep_hbm, mats_hbm, conv_hbm, a_row, skip, place, payload,
+    grad_out, third, states_hbm, back_toep_hbm, mats_hbm, conv_hbm, a_row, skip, place,
     mixed, small, mats, conv,
-    back_toep, g_cat, states, leave, sems,
+    g_cat, states, back_toep, leave, sems,
 ):
-    mats_in, toep_in, conv_in = begin(
-        [(mats_hbm, mats), (back_toep_hbm, back_toep), (conv_hbm, conv)], sems
+    states_in, mats_in, toep_in, conv_in = begin(
+        [(states_hbm, states), (mats_hbm, mats), (back_toep_hbm, back_toep), (conv_hbm, conv)], sems
     )
     a = a_row[...]
-    token = iota((128, 128), 0).astype(F32)
     wide = jnp.broadcast_to(a, (8, 128)) * float(LENGTH)
     is_state = iota((8, 128), 1) < 64
     me = place[0]
@@ -264,16 +253,16 @@
             c = slice(g * WIDTH, (g + 1) * WIDTH)
             g_cat[at, pl.ds(256 * g, 128)] = hi[c]
             g_cat[at, pl.ds(256 * g + 128, 128)] = lo[c]
-    states[...] = halves(dot(g_cat[...], state_matrix(a, token + 1.0)))
+    lane = iota((WIDTH, 128), 1)
+    finish([states_in])
     step = jnp.exp(-a * 128.0)
     carry = jnp.zeros((WIDTH, 128), F32)
     for n in reversed(range(SPANS)):
         at = pl.ds(n * WIDTH, WIDTH)
-        leave[at, :] = carry
+        leave[at, :] = quad_split(carry, lane)
         carry = carry * step + states[at, :]
-    lane = iota((ROWS, 128), 1)
     finish([mats_in])
-    mixed[...] = dot(quad_split(leave[...], lane), mats[1])
+    mixed[...] = dot(leave[...], mats[1])
     finish([toep_in])
     for g in range(GROUPS):
         here = pl.ds(128 * g, 128)
@@ -420,7 +409,8 @@
         out_shape=tuple(placed(kind, s, d) for kind, (s, d) in zip(kinds, outs)),
         in_specs=[pl.BlockSpec(memory_space=space(i)) for i in range(len(args))],
         out_specs=tuple(pl.BlockSpec(memory_space=kind) for kind in kinds),
-        scratch_shapes=[pltpu.VMEM(s, d) for s, d in scratch] + [pltpu.SemaphoreType.DMA((copies,))],
+        scratch_shapes=[pltpu.VMEM(s, d) for s, d in scratch]
+        + [pltpu.SemaphoreType.DMA((copies,))] * (copies > 0),
         compiler_params=pltpu.CompilerParams(vmem_limit_bytes=40 << 20),
     )(*(pinned(i, x) for i, x in enumerate(args)))
 
@@ -440,53 +430,55 @@
 WHOLE = ((ROWS, 256), F32)
 STATES = ((ROWS, 128), F32)
 ENTER = ((ROWS, 128), BF16)
+PAIRS = ((ROWS // 2, 128), BF16)
 EDGE = ((WIDTH + 8, 128), F32)
 TOEP = ((GROUPS, 256, 256), BF16)
 MATS = ((2, 128, 256), BF16)
 PARTS = ((CTX, 16, 128), F32)
 SMALL = ((2 * CTX + 1, 8, 128), F32)
+DECAYS = ((2, SPANS, 128), F32)
 RESIDUE = ((GROUPS, MODES), F32)
 SKIP = ((1, GROUPS * WIDTH), F32)
 
 
 def local(first, second, third, grad_out, exchange, residue, decay_rate, skip_gain, place):
     a_row, a_col, w_col, weight, skip = prepare(residue, decay_rate, skip_gain)
-    x_turn, enter, edge, third, x_cat, conv, back_toep, mats = call(
+    x_turn, edge, third, gated, pairs, conv, back_toep, mats = call(
         forward_kernel,
-        [TURN, ENTER, EDGE, GATE, CAT, WHOLE, TOEP, MATS],
-        [GATE, GATE, CAT, WHOLE, TOEP, MATS, STATES, TOEP],
-        7,
+        [TURN, EDGE, GATE, WHOLE, PAIRS, WHOLE, TOEP, MATS],
+        [GATE, GATE, CAT, ENTER, WHOLE, TOEP, MATS, STATES, TOEP],
+        6,
         (first, second, third, a_row, a_col, w_col, decay_rate, weight, skip),
         vmem=(3, 4, 5, 8),
         smem=(6, 7),
-        outs_near=(0, 1, 2, 3),
-    )
-    (payload,) = call(
+        outs_near=(0, 1, 2, 3, 4),
+    )
+    payload, states = call(
         middle_kernel,
-        [PARTS],
-        [CAT, CAT, STATES],
+        [PARTS, STATES],
+        [CAT, STATES],
         1,
-        (grad_out, third, x_turn, enter, edge, x_cat),
-        near=(0, 1, 2, 3, 4),
+        (grad_out, third, x_turn, edge, gated, pairs),
+        near=(0, 1, 2, 3, 4, 5),
         outs_near=(0,),
     )
     parts = exchange(payload)
     mixed, small, mats, conv = call(
         backward_kernel,
         [WHOLE, SMALL, MATS, WHOLE],
-        [TOEP, CAT, STATES, STATES],
-        3,
-        (grad_out, third, back_toep, mats, conv, a_row, skip, place, payload),
-        near=(0, 1, 8),
-        vmem=(5, 6),
-        smem=(7,),
+        [CAT, STATES, TOEP, ENTER],
+        4,
+        (grad_out, third, states, back_toep, mats, conv, a_row, skip, place),
+        near=(0, 1),
+        vmem=(6, 7),
+        smem=(8,),
         outs_near=(0, 1, 2, 3),
     )
     outs = [GATE, GATE, GATE, RESIDUE, SKIP]
     grad_first, grad_second, grad_third, grad_residue, grad_skip = call(
         finish_kernel,
         outs,
-        [GATE, GATE] + outs + [((2, SPANS, 128), F32)],
+        [GATE, GATE] + outs + [DECAYS],
         FINISH_COPIES,
         (parts, small, mats, conv, mixed, grad_out, first, second),
         near=(0, 1, 2, 3, 4, 5),

time: 66.9 us -> 65.8 us (0.984)
  Pallas kernels: 14.4 us -> 13 us
    pallas_call x1 -> x0, Pallas kernels: 1.94 us -> none  [swap(): pl.pallas_call(swap_kernel, out_shape=pltpu.VMEM(heads.shape, heads.dtype...]
    pallas_call x4 -> x5, Pallas kernels: 12.4 us -> 13 us  [call(): pl.pallas_call(kernel, out_shape=tuple((placed(kind, s, d) for kind, (s,...]
  transfers between devices with their start and end apart: 2 -> 2, of which waited for: 1 -> 2; matrix products, arithmetic and copies ran while one was open for 1% -> 1% of each run, Pallas kernels for 11% -> 10%
where the time goes in v5:
time: 65.8 us; the launch traced here: 65.4 us
  starting transfers between devices  32.4 us (49%)
  waiting for transfers between devices  17.5 us (27%)
  Pallas kernels  13 us (20%)
  local copies, waits for them, and re-layouts  1.71 us (3%)
  between operations  0.72 us (1%)
    all_to_all x1, starting transfers between devices, on_device(): lax.all_to_all(swap(grad_heads.reshape(SPANS, GROUPS * WIDTH, SPAN)), 'ch...  17.8 us
    all_to_all x1, waiting for transfers between devices, on_device(): lax.all_to_all(swap(grad_heads.reshape(SPANS, GROUPS * WIDTH, SPAN)), 'ch...  17.4 us
    all_to_all x1, starting transfers between devices, exchange(): lax.all_to_all(payload, 'ctx', split_axis=0, concat_axis=0, tiled=True, a...  14.6 us
    pallas_call x5, Pallas kernels, call(): pl.pallas_call(kernel, out_shape=tuple((placed(kind, s, d) for kind, (s,...  13 us
  transfers between devices with their start and end apart: 2, of which 2 were waited for; matrix products, arithmetic and copies ran while one was open for 1% of the time, Pallas kernels for 10%

profile of v5, /device:TPU:1, one launch (start us, length us, event | category | flops | bytes accessed | tf_op | source)
XLA Modules:
  0.0 65.4 jit_solution(9994432285760833046)
XLA Ops:
  0.6 1.9 %shard_map.110 = bf16[64,32,128]{2,1,0:T(8,128)(2,1)} custom-call(bf16[64,32,128]{2,1,0:T(8,128)(2,1)} %bitcast.3), custom_call_target="tpu_custom_call" | custom-call | tf_op jit(solution)/shard_map/pallas_call | solution.py:407
  2.6 0.0 copy-start
  2.6 17.8 %all-to-all-start = ((bf16[64,32,128]{2,1,0:T(8,128)(2,1)}), bf16[64,32,128]{2,1,0:T(8,128)(2,1)S(1)}, u32[]{:S(2)}, u32[]{:S(2)}) async-start(bf16[64,32,128]{2,1,0:T(8,128)(2,1)} %shard_map.110), calls=%async_computation | async-start | bytes 1048576 | tf_op jit(solution)/shard_map/all_to_all | solution.py:490
  20.4 0.0 copy-done
  20.4 0.1 tile.26
  20.5 0.1 tile.28.a_row
  20.6 0.0 copy-start.1
  20.6 0.1 tile.33.a_col
  20.7 0.6 copy-done.1
  21.3 0.0 copy-start.2
  21.3 0.1 tile.30
  21.4 0.6 copy-done.2
  21.9 0.1 reshape.44.skip
  22.1 0.1 tile.34.w_col
  22.2 4.3 %shard_map.111 = (bf16[2,256,1024]{2,1,0:T(8,128)(2,1)S(1)}, f32[24,128]{1,0:T(8,128)S(1)}, bf16[32,8192]{1,0:T(8,128)(2,1)S(1)}, f32[1024,256]{1,0:T(8,128)S(1)...) custom-call(bf16[32,8192]{1,0:T(8,128)(2,1)} %first_hbm.3, ...), custom_call_target="tpu_custom_call" | custom-call | tf_op jit(solution)/shard_map/pallas_call | solution.py:407
  26.5 17.4 %all-to-all-done.grad_out = bf16[64,32,128]{2,1,0:T(8,128)(2,1)S(1)} async-done(((bf16[64,32,128]{2,1,0:T(8,128)(2,1)}), bf16[64,32,128]{2,1,0:T(8,128)(2,1)S(1)}, u32[]{:S(2)}, u32[]{:S(2)}) %all-to-all-start) | async-done | bytes 524320 | tf_op jit(solution)/shard_map/all_to_all | solution.py:490
  43.9 2.2 %shard_map.112 = (f32[8,16,128]{2,1,0:T(8,128)}, f32[1024,128]{1,0:T(8,128)}) custom-call(bf16[64,32,128]{2,1,0:T(8,128)(2,1)S(1)} %all-to-all-done.grad_out, bf16[32,8192]{1,0:T(8,128)(2,1)S(1)} %get-tuple-element.24.third, bf16[2,256,1024]{2,1,0:T(8,128)(2,1)S(1)} %get-tuple-element.25.x_turn, f32[24,128]{1,0:T(8,128)S(1)} %get-tuple-element.26.edge, ...), custom_call_target="tpu_custom_call" | custom-call | tf_op jit(solution)/shard_map/pallas_call | solution.py:407
  46.2 14.6 %all-to-all-start.1 = ((f32[8,16,128]{2,1,0:T(8,128)}), f32[8,16,128]{2,1,0:T(8,128)S(1)}, u32[]{:S(2)}, u32[]{:S(2)}) async-start(f32[8,16,128]{2,1,0:T(8,128)} %get-tuple-element.29), calls=%async_computation.1 | async-start | bytes 131072 | tf_op jit(solution)/shard_map/all_to_all | solution.py:501
  60.7 2.0 %shard_map.113 = (f32[1024,256]{1,0:T(8,128)S(1)}, f32[17,8,128]{2,1,0:T(8,128)S(1)}, bf16[2,128,256]{2,1,0:T(8,128)(2,1)S(1)}, f32[1024,256]{1,0:T(8,128)S(1)}) custom-call(bf16[64,32,128]{2,1,0:T(8,128)(2,1)S(1)} %all-to-all-done.grad_out, bf16[32,8192]{1,0:T(8,128)(2,1)S(1)} %get-tuple-element.24.third, f32[1024,128]{1,0:T(8,128)} %get-tuple-element.30.states_hbm, ...), custom_call_target="tpu_custom_call" | custom-call | tf_op jit(solution)/shard_map/pallas_call | solution.py:407
  62.7 0.1 all-to-all-done.1.parts
  62.8 2.6 %shard_map.114 = (bf16[32,8192]{1,0:T(8,128)(2,1)}, bf16[32,8192]{1,0:T(8,128)(2,1)}, bf16[32,8192]{1,0:T(8,128)(2,1)}, f32[2,16]{1,0:T(2,128)}, f32[1,32]{1,0:T(1,128)}) custom-call(f32[8,16,128]{2,1,0:T(8,128)S(1)} %all-to-all-done.1.parts, f32[17,8,128]{2,1,0:T(8,128)S(1)} %get-tuple-element.34.small, bf16[2,128,256]{2,1,0:T(8,128)(2,1)S(1)} %get-tuple-element.35.mats, ...), custom_call_target="tpu_custom_call" | custom-call | tf_op jit(solution)/shard_map/pallas_call | solution.py:407
  (3 shorter events, 0.0 us)
Async XLA Ops:
  2.6 17.9 %copy-start = (f32[2,16]{1,0:T(2,128)S(1)}, f32[2,16]{1,0:T(2,128)}, u32[]{:S(2)}) copy-start(f32[2,16]{1,0:T(2,128)} %a_s.1) | copy-start | bytes 388
  2.6 41.4 %all-to-all-start = ((bf16[64,32,128]{2,1,0:T(8,128)(2,1)}), bf16[64,32,128]{2,1,0:T(8,128)(2,1)S(1)}, u32[]{:S(2)}, u32[]{:S(2)}) async-start(bf16[64,32,128]{2,1,0:T(8,128)(2,1)} %shard_map.110), calls=%async_computation | async-start | bytes 1048576 | tf_op jit(solution)/shard_map/all_to_all | solution.py:490
  20.6 0.7 %copy-start.1 = (f32[2,16]{1,0:T(2,128)S(1)}, f32[2,16]{1,0:T(2,128)}, u32[]{:S(2)}) copy-start(f32[2,16]{1,0:T(2,128)} %param.11) | copy-start | bytes 388
  21.3 0.7 %copy-start.2 = (f32[32]{0:T(128)S(1)}, f32[32]{0:T(128)}, u32[]{:S(2)}) copy-start(f32[32]{0:T(128)} %param.13) | copy-start | bytes 388
  46.2 16.6 %all-to-all-start.1 = ((f32[8,16,128]{2,1,0:T(8,128)}), f32[8,16,128]{2,1,0:T(8,128)S(1)}, u32[]{:S(2)}, u32[]{:S(2)}) async-start(f32[8,16,128]{2,1,0:T(8,128)} %get-tuple-element.29), calls=%async_computation.1 | async-start | bytes 131072 | tf_op jit(solution)/shard_map/all_to_all | solution.py:501

commit v6 on v5

--- a/solution.py
+++ b/solution.py
@@ -146,8 +146,8 @@
 CTX_ORDER = [5, 1, 3, 7, 2, 0, 4, 6]
 CTX_PLACE = [CTX_ORDER.index(k) for k in range(CTX)]
 RUNS = [(0, 1), (FIRST, FIRST + 1)]
-RUNS += [(i, min(i + 9, FIRST)) for i in range(1, FIRST, 9)]
-RUNS += [(i, min(i + 9, SPANS)) for i in range(FIRST + 1, SPANS, 9)]
+RUNS += [(i, min(i + 22, FIRST)) for i in range(1, FIRST, 22)]
+RUNS += [(i, min(i + 22, SPANS)) for i in range(FIRST + 1, SPANS, 22)]
 
 
 def swap_kernel(heads, swapped, held, sems):
@@ -168,8 +168,8 @@
 
 def middle_kernel(
     grad_out, third, x_turn, edge, gated, pairs,
-    payload, states_hbm,
-    g_cat, states, sems,
+    payload_hbm, states_hbm,
+    g_cat, states, payload, sems,
 ):
     row = iota((128, 128), 0)
     col = iota((128, 128), 1)
@@ -222,7 +222,7 @@
     for k in range(CTX):
         payload[k, :8, :] = back
         payload[k, 8:, :] = ahead
-    finish(outputs)
+    finish(outputs + begin([(payload, payload_hbm)], sems, 1))
 
 
 def backward_kernel(
@@ -273,40 +273,13 @@
     finish([conv_in])
 
 
-CHUNKS = 4
-CHUNK_SPANS = SPANS // CHUNKS
-CHUNK_ROWS = ROWS // CHUNKS
-CHUNK_TOKENS = LENGTH // CHUNKS
-
-
 def finish_kernel(
     parts, small, mats, conv, mixed, grad_out, first_hbm, second_hbm,
     grad_first_hbm, grad_second_hbm, grad_third_hbm, grad_residue_hbm, grad_skip_hbm,
-    first, second, grad_first, grad_second, grad_third, grad_residue, grad_skip, decays,
+    first, second, grad_first, grad_second, grad_third, grad_residue, grad_skip, decays, left, result,
     sems,
 ):
-    def rows_of(c):
-        return pl.ds(c * CHUNK_ROWS, CHUNK_ROWS)
-
-    def spans_of(c):
-        return pl.ds(c * CHUNK_SPANS, CHUNK_SPANS)
-
-    def tokens_of(c):
-        return pl.ds(c * CHUNK_TOKENS, CHUNK_TOKENS)
-
-    gate_in = []
-    for c in range(CHUNKS):
-        gate_in.append(
-            begin(
-                [
-                    (first_hbm.at[:, tokens_of(c)], first.at[:, tokens_of(c)]),
-                    (second_hbm.at[:, tokens_of(c)], second.at[:, tokens_of(c)]),
-                ],
-                sems,
-                2 * c,
-            )
-        )
-    used = 2 * CHUNKS
+    gates_in = begin([(first_hbm, first), (second_hbm, second)], sems)
     a = small[2 * CTX, 0:1, :]
     quarter = iota((8, 128), 1) // 32
     back = jnp.zeros((8, 128), F32)
@@ -333,27 +306,22 @@
     span = iota((SPANS, 128), 0).astype(F32)
     decays[0] = jnp.exp(-a * (128.0 * span))
     decays[1] = jnp.exp(-a * (128.0 * (SPANS - 1.0 - span)))
-    lane = iota((CHUNK_ROWS, 128), 1)
-
-    def fix(x, side, c):
-        decay = decays[side, spans_of(c), :].reshape(CHUNK_SPANS, 1, 128)
-        whole = (decay * x.reshape(1, WIDTH, 128)).reshape(CHUNK_ROWS, 128)
-        return dot(quad_split(whole, lane), mats[side])
-
-    def channels(x, i):
-        x = x[i * WIDTH : (i + 1) * WIDTH]
-        return jnp.concatenate([x[:, :128], x[:, 128:]], axis=0)
-
+    lane = iota((ROWS, 128), 1)
+
+    def fix(x, side):
+        whole = (decays[side].reshape(SPANS, 1, 128) * x.reshape(1, WIDTH, 128)).reshape(ROWS, 128)
+        left[...] = quad_split(whole, lane)
+        return dot(left[...], mats[side])
+
+    result[...] = conv[...] + fix(rows(ahead), 0)
     outputs = []
-    entering, leaving = rows(ahead), rows(back)
-    for c in range(CHUNKS):
-        add = fix(entering, 0, c)
-        full = conv[rows_of(c), :] + add
-        for i in range(CHUNK_SPANS):
-            n = c * CHUNK_SPANS + i
-            grad_third[:, pl.ds(n * SPAN, SPAN)] = (grad_out[CH_ORDER[n]].astype(F32) * channels(full, i)).astype(BF16)
-        outputs += begin([(grad_third.at[:, tokens_of(c)], grad_third_hbm.at[:, tokens_of(c)])], sems, used)
-        used += 1
+    for g in range(GROUPS):
+        mine = pl.ds(g * WIDTH, WIDTH)
+        for n in range(SPANS):
+            full = result[pl.ds(n * WIDTH, WIDTH), pl.ds(128 * g, 128)]
+            heads = grad_out[CH_ORDER[n], mine, :].astype(F32)
+            grad_third[mine, pl.ds(n * SPAN, SPAN)] = (heads * full).astype(BF16)
+        outputs += begin([(grad_third.at[mine, :], grad_third_hbm.at[mine, :])], sems, 2 + g)
     near = spread(back, 2)
     crossed = (spread(far, 0) + spread(far, 1)) * jnp.exp(a)
     weight = jnp.sum(near + crossed, axis=0, keepdims=True)
@@ -362,30 +330,28 @@
     grad_residue[1:2, :] = pltpu.roll(weight, 128 - MODES, 1)[:, :MODES]
     direct = pltpu.roll(back, 32, 1)[0:1] * (1.0 / (float(TOKENS) ** 0.5))
     grad_skip[...] = direct[:, : GROUPS * WIDTH]
-    outputs += begin([(grad_residue, grad_residue_hbm), (grad_skip, grad_skip_hbm)], sems, used)
-    used += 2
-    for c in range(CHUNKS):
-        add = fix(leaving, 1, c)
-        finish(gate_in[c])
-        full = mixed[rows_of(c), :] + add
-        for i in range(CHUNK_SPANS):
-            here = pl.ds((c * CHUNK_SPANS + i) * SPAN, SPAN)
-            part = channels(full, i)
-            grad_first[:, here] = (part * second[:, here].astype(F32)).astype(BF16)
-            grad_second[:, here] = (part * first[:, here].astype(F32)).astype(BF16)
+    outputs += begin([(grad_residue, grad_residue_hbm), (grad_skip, grad_skip_hbm)], sems, 4)
+    result[...] = mixed[...] + fix(rows(back), 1)
+    finish(gates_in)
+    for g in range(GROUPS):
+        mine = pl.ds(g * WIDTH, WIDTH)
+        for n in range(SPANS):
+            here = pl.ds(n * SPAN, SPAN)
+            part = result[pl.ds(n * WIDTH, WIDTH), pl.ds(128 * g, 128)]
+            grad_first[mine, here] = (part * second[mine, here].astype(F32)).astype(BF16)
+            grad_second[mine, here] = (part * first[mine, here].astype(F32)).astype(BF16)
         outputs += begin(
             [
-                (grad_first.at[:, tokens_of(c)], grad_first_hbm.at[:, tokens_of(c)]),
-                (grad_second.at[:, tokens_of(c)], grad_second_hbm.at[:, tokens_of(c)]),
+                (grad_first.at[mine, :], grad_first_hbm.at[mine, :]),
+                (grad_second.at[mine, :], grad_second_hbm.at[mine, :]),
             ],
             sems,
-            used,
+            6 + 2 * g,
         )
-        used += 2
     finish(outputs)
 
 
-FINISH_COPIES = 2 * CHUNKS + 3 * CHUNKS + 2
+FINISH_COPIES = 10
 
 
 def placed(kind, shape, dtype):
@@ -456,11 +422,10 @@
     payload, states = call(
         middle_kernel,
         [PARTS, STATES],
-        [CAT, STATES],
-        1,
+        [CAT, STATES, PARTS],
+        2,
         (grad_out, third, x_turn, edge, gated, pairs),
         near=(0, 1, 2, 3, 4, 5),
-        outs_near=(0,),
     )
     parts = exchange(payload)
     mixed, small, mats, conv = call(
@@ -478,7 +443,7 @@
     grad_first, grad_second, grad_third, grad_residue, grad_skip = call(
         finish_kernel,
         outs,
-        [GATE, GATE] + outs + [DECAYS],
+        [GATE, GATE] + outs + [DECAYS, ENTER, WHOLE],
         FINISH_COPIES,
         (parts, small, mats, conv, mixed, grad_out, first, second),
         near=(0, 1, 2, 3, 4, 5),

time: 65.8 us -> 64.9 us (0.986)
  Pallas kernels: 13 us -> 12.1 us
    pallas_call x5, Pallas kernels: 13 us -> 12.1 us  [call(): pl.pallas_call(kernel, out_shape=tuple((placed(kind, s, d) for kind, (s,...]
where the time goes in v6:
time: 64.9 us; the launch traced here: 64.5 us
  starting transfers between devices  32.4 us (50%)
  waiting for transfers between devices  17.5 us (27%)
  Pallas kernels  12.1 us (19%)
  local copies, waits for them, and re-layouts  1.71 us (3%)
  between operations  0.72 us (1%)
    all_to_all x1, starting transfers between devices, on_device(): lax.all_to_all(swap(grad_heads.reshape(SPANS, GROUPS * WIDTH, SPAN)), 'ch...  17.8 us
    all_to_all x1, waiting for transfers between devices, on_device(): lax.all_to_all(swap(grad_heads.reshape(SPANS, GROUPS * WIDTH, SPAN)), 'ch...  17.4 us
    all_to_all x1, starting transfers between devices, exchange(): lax.all_to_all(payload, 'ctx', split_axis=0, concat_axis=0, tiled=True, a...  14.6 us
    pallas_call x5, Pallas kernels, call(): pl.pallas_call(kernel, out_shape=tuple((placed(kind, s, d) for kind, (s,...  12.1 us
  transfers between devices with their start and end apart: 2, of which 2 were waited for; matrix products, arithmetic and copies ran while one was open for 1% of the time, Pallas kernels for 10%

profile of v6, /device:TPU:1, one launch (start us, length us, event | category | flops | bytes accessed | tf_op | source)
XLA Modules:
  0.0 64.5 jit_solution(4593096015793748291)
XLA Ops:
  0.6 1.9 %shard_map.110 = bf16[64,32,128]{2,1,0:T(8,128)(2,1)} custom-call(bf16[64,32,128]{2,1,0:T(8,128)(2,1)} %bitcast.3), custom_call_target="tpu_custom_call" | custom-call | tf_op jit(solution)/shard_map/pallas_call | solution.py:373
  2.5 0.0 copy-start
  2.5 17.8 %all-to-all-start = ((bf16[64,32,128]{2,1,0:T(8,128)(2,1)}), bf16[64,32,128]{2,1,0:T(8,128)(2,1)S(1)}, u32[]{:S(2)}, u32[]{:S(2)}) async-start(bf16[64,32,128]{2,1,0:T(8,128)(2,1)} %shard_map.110), calls=%async_computation | async-start | bytes 1048576 | tf_op jit(solution)/shard_map/all_to_all | solution.py:455
  20.4 0.0 copy-done
  20.4 0.1 tile.26
  20.5 0.1 tile.28.a_row
  20.5 0.0 copy-start.1
  20.5 0.1 tile.33.a_col
  20.7 0.6 copy-done.1
  21.2 0.0 copy-start.2
  21.2 0.1 tile.30
  21.3 0.6 copy-done.2
  21.9 0.1 reshape.44.skip
  22.0 0.1 tile.34.w_col
  22.1 4.3 %shard_map.111 = (bf16[2,256,1024]{2,1,0:T(8,128)(2,1)S(1)}, f32[24,128]{1,0:T(8,128)S(1)}, bf16[32,8192]{1,0:T(8,128)(2,1)S(1)}, f32[1024,256]{1,0:T(8,128)S(1)...) custom-call(bf16[32,8192]{1,0:T(8,128)(2,1)} %first_hbm.3, ...), custom_call_target="tpu_custom_call" | custom-call | tf_op jit(solution)/shard_map/pallas_call | solution.py:373
  26.4 17.4 %all-to-all-done.grad_out = bf16[64,32,128]{2,1,0:T(8,128)(2,1)S(1)} async-done(((bf16[64,32,128]{2,1,0:T(8,128)(2,1)}), bf16[64,32,128]{2,1,0:T(8,128)(2,1)S(1)}, u32[]{:S(2)}, u32[]{:S(2)}) %all-to-all-start) | async-done | bytes 524320 | tf_op jit(solution)/shard_map/all_to_all | solution.py:455
  43.9 1.7 %shard_map.112 = (f32[8,16,128]{2,1,0:T(8,128)}, f32[1024,128]{1,0:T(8,128)}) custom-call(bf16[64,32,128]{2,1,0:T(8,128)(2,1)S(1)} %all-to-all-done.grad_out, bf16[32,8192]{1,0:T(8,128)(2,1)S(1)} %get-tuple-element.24.third, bf16[2,256,1024]{2,1,0:T(8,128)(2,1)S(1)} %get-tuple-element.25.x_turn, f32[24,128]{1,0:T(8,128)S(1)} %get-tuple-element.26.edge, ...), custom_call_target="tpu_custom_call" | custom-call | tf_op jit(solution)/shard_map/pallas_call | solution.py:373
  45.6 14.6 %all-to-all-start.1 = ((f32[8,16,128]{2,1,0:T(8,128)}), f32[8,16,128]{2,1,0:T(8,128)S(1)}, u32[]{:S(2)}, u32[]{:S(2)}) async-start(f32[8,16,128]{2,1,0:T(8,128)} %get-tuple-element.29), calls=%async_computation.1 | async-start | bytes 131072 | tf_op jit(solution)/shard_map/all_to_all | solution.py:466
  60.1 2.0 %shard_map.113 = (f32[1024,256]{1,0:T(8,128)S(1)}, f32[17,8,128]{2,1,0:T(8,128)S(1)}, bf16[2,128,256]{2,1,0:T(8,128)(2,1)S(1)}, f32[1024,256]{1,0:T(8,128)S(1)}) custom-call(bf16[64,32,128]{2,1,0:T(8,128)(2,1)S(1)} %all-to-all-done.grad_out, bf16[32,8192]{1,0:T(8,128)(2,1)S(1)} %get-tuple-element.24.third, f32[1024,128]{1,0:T(8,128)} %get-tuple-element.30.states_hbm, ...), custom_call_target="tpu_custom_call" | custom-call | tf_op jit(solution)/shard_map/pallas_call | solution.py:373
  62.1 0.1 all-to-all-done.1.parts
  62.2 2.3 %shard_map.114 = (bf16[32,8192]{1,0:T(8,128)(2,1)}, bf16[32,8192]{1,0:T(8,128)(2,1)}, bf16[32,8192]{1,0:T(8,128)(2,1)}, f32[2,16]{1,0:T(2,128)}, f32[1,32]{1,0:T(1,128)}) custom-call(f32[8,16,128]{2,1,0:T(8,128)S(1)} %all-to-all-done.1.parts, f32[17,8,128]{2,1,0:T(8,128)S(1)} %get-tuple-element.34.small, bf16[2,128,256]{2,1,0:T(8,128)(2,1)S(1)} %get-tuple-element.35.mats, ...), custom_call_target="tpu_custom_call" | custom-call | tf_op jit(solution)/shard_map/pallas_call | solution.py:373
  (3 shorter events, 0.0 us)
Async XLA Ops:
  2.5 17.9 %copy-start = (f32[2,16]{1,0:T(2,128)S(1)}, f32[2,16]{1,0:T(2,128)}, u32[]{:S(2)}) copy-start(f32[2,16]{1,0:T(2,128)} %a_s.1) | copy-start | bytes 388
  2.5 41.4 %all-to-all-start = ((bf16[64,32,128]{2,1,0:T(8,128)(2,1)}), bf16[64,32,128]{2,1,0:T(8,128)(2,1)S(1)}, u32[]{:S(2)}, u32[]{:S(2)}) async-start(bf16[64,32,128]{2,1,0:T(8,128)(2,1)} %shard_map.110), calls=%async_computation | async-start | bytes 1048576 | tf_op jit(solution)/shard_map/all_to_all | solution.py:455
  20.5 0.7 %copy-start.1 = (f32[2,16]{1,0:T(2,128)S(1)}, f32[2,16]{1,0:T(2,128)}, u32[]{:S(2)}) copy-start(f32[2,16]{1,0:T(2,128)} %param.11) | copy-start | bytes 388
  21.2 0.7 %copy-start.2 = (f32[32]{0:T(128)S(1)}, f32[32]{0:T(128)}, u32[]{:S(2)}) copy-start(f32[32]{0:T(128)} %param.13) | copy-start | bytes 388
  45.6 16.6 %all-to-all-start.1 = ((f32[8,16,128]{2,1,0:T(8,128)}), f32[8,16,128]{2,1,0:T(8,128)S(1)}, u32[]{:S(2)}, u32[]{:S(2)}) async-start(f32[8,16,128]{2,1,0:T(8,128)} %get-tuple-element.29), calls=%async_computation.1 | async-start | bytes 131072 | tf_op jit(solution)/shard_map/all_to_all | solution.py:466

commit v7 on v6

--- a/solution.py
+++ b/solution.py
@@ -207,11 +207,11 @@
     far = far[:8] + far[8:]
     far = far + pltpu.roll(far, 32, 1)
     weight = near + (far + pltpu.roll(far, 64, 1)) * jnp.exp(a)
+    sums = jnp.concatenate(total * 4, axis=0)
     direct = lax.dot_general(
-        jnp.ones((8, SPAN), F32),
-        jnp.concatenate(total * 4, axis=0),
+        jnp.ones((8, 2 * SPAN), BF16),
+        jnp.concatenate([high(sums), low(sums)], axis=1),
         (((1,), (1,)), ((), ())),
-        precision=lax.Precision.HIGHEST,
         preferred_element_type=F32,
     )
     quarter = iota((8, 128), 1) // 32

time: 64.9 us -> 64.8 us (level)
  no operation moved by 1% of the time
where the time goes in v7:
time: 64.8 us; the launch traced here: 64.4 us
  starting transfers between devices  32.4 us (50%)
  waiting for transfers between devices  17.5 us (27%)
  Pallas kernels  12.1 us (19%)
  local copies, waits for them, and re-layouts  1.71 us (3%)
  between operations  0.72 us (1%)
    all_to_all x1, starting transfers between devices, on_device(): lax.all_to_all(swap(grad_heads.reshape(SPANS, GROUPS * WIDTH, SPAN)), 'ch...  17.8 us
    all_to_all x1, waiting for transfers between devices, on_device(): lax.all_to_all(swap(grad_heads.reshape(SPANS, GROUPS * WIDTH, SPAN)), 'ch...  17.4 us
    all_to_all x1, starting transfers between devices, exchange(): lax.all_to_all(payload, 'ctx', split_axis=0, concat_axis=0, tiled=True, a...  14.6 us
    pallas_call x5, Pallas kernels, call(): pl.pallas_call(kernel, out_shape=tuple((placed(kind, s, d) for kind, (s,...  12.1 us
  transfers between devices with their start and end apart: 2, of which 2 were waited for; matrix products, arithmetic and copies ran while one was open for 1% of the time, Pallas kernels for 10%

profile of v7, /device:TPU:1, one launch (start us, length us, event | category | flops | bytes accessed | tf_op | source)
XLA Modules:
  0.0 64.4 jit_solution(7745440136792190302)
XLA Ops:
  0.6 1.9 %shard_map.110 = bf16[64,32,128]{2,1,0:T(8,128)(2,1)} custom-call(bf16[64,32,128]{2,1,0:T(8,128)(2,1)} %bitcast.3), custom_call_target="tpu_custom_call" | custom-call | tf_op jit(solution)/shard_map/pallas_call | solution.py:373
  2.5 0.0 copy-start
  2.5 17.8 %all-to-all-start = ((bf16[64,32,128]{2,1,0:T(8,128)(2,1)}), bf16[64,32,128]{2,1,0:T(8,128)(2,1)S(1)}, u32[]{:S(2)}, u32[]{:S(2)}) async-start(bf16[64,32,128]{2,1,0:T(8,128)(2,1)} %shard_map.110), calls=%async_computation | async-start | bytes 1048576 | tf_op jit(solution)/shard_map/all_to_all | solution.py:455
  20.4 0.0 copy-done
  20.4 0.1 tile.26
  20.5 0.1 tile.28.a_row
  20.5 0.0 copy-start.1
  20.5 0.1 tile.33.a_col
  20.7 0.6 copy-done.1
  21.2 0.0 copy-start.2
  21.2 0.1 tile.30
  21.3 0.6 copy-done.2
  21.9 0.1 reshape.44.skip
  22.0 0.1 tile.34.w_col
  22.1 4.3 %shard_map.111 = (bf16[2,256,1024]{2,1,0:T(8,128)(2,1)S(1)}, f32[24,128]{1,0:T(8,128)S(1)}, bf16[32,8192]{1,0:T(8,128)(2,1)S(1)}, f32[1024,256]{1,0:T(8,128)S(1)...) custom-call(bf16[32,8192]{1,0:T(8,128)(2,1)} %first_hbm.3, ...), custom_call_target="tpu_custom_call" | custom-call | tf_op jit(solution)/shard_map/pallas_call | solution.py:373
  26.4 17.4 %all-to-all-done.grad_out = bf16[64,32,128]{2,1,0:T(8,128)(2,1)S(1)} async-done(((bf16[64,32,128]{2,1,0:T(8,128)(2,1)}), bf16[64,32,128]{2,1,0:T(8,128)(2,1)S(1)}, u32[]{:S(2)}, u32[]{:S(2)}) %all-to-all-start) | async-done | bytes 524320 | tf_op jit(solution)/shard_map/all_to_all | solution.py:455
  43.9 1.6 %shard_map.112 = (f32[8,16,128]{2,1,0:T(8,128)}, f32[1024,128]{1,0:T(8,128)}) custom-call(bf16[64,32,128]{2,1,0:T(8,128)(2,1)S(1)} %all-to-all-done.grad_out, bf16[32,8192]{1,0:T(8,128)(2,1)S(1)} %get-tuple-element.24.third, bf16[2,256,1024]{2,1,0:T(8,128)(2,1)S(1)} %get-tuple-element.25.x_turn, f32[24,128]{1,0:T(8,128)S(1)} %get-tuple-element.26.edge, ...), custom_call_target="tpu_custom_call" | custom-call | tf_op jit(solution)/shard_map/pallas_call | solution.py:373
  45.5 14.6 %all-to-all-start.1 = ((f32[8,16,128]{2,1,0:T(8,128)}), f32[8,16,128]{2,1,0:T(8,128)S(1)}, u32[]{:S(2)}, u32[]{:S(2)}) async-start(f32[8,16,128]{2,1,0:T(8,128)} %get-tuple-element.29), calls=%async_computation.1 | async-start | bytes 131072 | tf_op jit(solution)/shard_map/all_to_all | solution.py:466
  60.1 2.0 %shard_map.113 = (f32[1024,256]{1,0:T(8,128)S(1)}, f32[17,8,128]{2,1,0:T(8,128)S(1)}, bf16[2,128,256]{2,1,0:T(8,128)(2,1)S(1)}, f32[1024,256]{1,0:T(8,128)S(1)}) custom-call(bf16[64,32,128]{2,1,0:T(8,128)(2,1)S(1)} %all-to-all-done.grad_out, bf16[32,8192]{1,0:T(8,128)(2,1)S(1)} %get-tuple-element.24.third, f32[1024,128]{1,0:T(8,128)} %get-tuple-element.30.states_hbm, ...), custom_call_target="tpu_custom_call" | custom-call | tf_op jit(solution)/shard_map/pallas_call | solution.py:373
  62.0 0.1 all-to-all-done.1.parts
  62.1 2.3 %shard_map.114 = (bf16[32,8192]{1,0:T(8,128)(2,1)}, bf16[32,8192]{1,0:T(8,128)(2,1)}, bf16[32,8192]{1,0:T(8,128)(2,1)}, f32[2,16]{1,0:T(2,128)}, f32[1,32]{1,0:T(1,128)}) custom-call(f32[8,16,128]{2,1,0:T(8,128)S(1)} %all-to-all-done.1.parts, f32[17,8,128]{2,1,0:T(8,128)S(1)} %get-tuple-element.34.small, bf16[2,128,256]{2,1,0:T(8,128)(2,1)S(1)} %get-tuple-element.35.mats, ...), custom_call_target="tpu_custom_call" | custom-call | tf_op jit(solution)/shard_map/pallas_call | solution.py:373
  (3 shorter events, 0.0 us)
Async XLA Ops:
  2.5 17.9 %copy-start = (f32[2,16]{1,0:T(2,128)S(1)}, f32[2,16]{1,0:T(2,128)}, u32[]{:S(2)}) copy-start(f32[2,16]{1,0:T(2,128)} %a_s.1) | copy-start | bytes 388
  2.5 41.4 %all-to-all-start = ((bf16[64,32,128]{2,1,0:T(8,128)(2,1)}), bf16[64,32,128]{2,1,0:T(8,128)(2,1)S(1)}, u32[]{:S(2)}, u32[]{:S(2)}) async-start(bf16[64,32,128]{2,1,0:T(8,128)(2,1)} %shard_map.110), calls=%async_computation | async-start | bytes 1048576 | tf_op jit(solution)/shard_map/all_to_all | solution.py:455
  20.5 0.7 %copy-start.1 = (f32[2,16]{1,0:T(2,128)S(1)}, f32[2,16]{1,0:T(2,128)}, u32[]{:S(2)}) copy-start(f32[2,16]{1,0:T(2,128)} %param.11) | copy-start | bytes 388
  21.2 0.7 %copy-start.2 = (f32[32]{0:T(128)S(1)}, f32[32]{0:T(128)}, u32[]{:S(2)}) copy-start(f32[32]{0:T(128)} %param.13) | copy-start | bytes 388
  45.5 16.6 %all-to-all-start.1 = ((f32[8,16,128]{2,1,0:T(8,128)}), f32[8,16,128]{2,1,0:T(8,128)S(1)}, u32[]{:S(2)}, u32[]{:S(2)}) async-start(f32[8,16,128]{2,1,0:T(8,128)} %get-tuple-element.29), calls=%async_computation.1 | async-start | bytes 131072 | tf_op jit(solution)/shard_map/all_to_all | solution.py:466
